TPU v7x, 32 devices: a whole 2x2x4 slice. The times are simulated.
32 devices in a mesh: groups: 2 (over y), latent: 8 (over z, x), hidden: 2 (over core).
Axes of the slice: x: 2, y: 2, z: 4, core: 2. Of those that a mesh axis runs over, the one named last changes fastest.
Arguments:
- input_codes: int32 [288, 2304], P('groups', ('latent', 'hidden')), parts along dimension 0, may hold values from -128 to 127
- cotangent_codes: int32 [288, 2304], P('groups', ('latent', 'hidden')), parts along dimension 0, may hold values from -128 to 127
- dictionary: bfloat16 [8192, 2304], P(('latent', 'hidden')), as said below
- encoder_bias: float32 [8192], P(('latent', 'hidden')), may hold values from -12 to 0, as said below
- decoder_bias: float32 [2304], replicated, may hold values from -1.2 to 1.2
- norm_gain: float32 [2304], replicated, may hold values from 0.1 to 1.9
- gate_weight: bfloat16 [8192, 2304], P(('latent', 'hidden')), may hold values from -0.1875 to 0.1875
- up_weight: bfloat16 [8192, 2304], P(('latent', 'hidden')), may hold values from -0.1875 to 0.1875
- down_weight: bfloat16 [8192, 2304], P(('latent', 'hidden')), may hold values from -0.09375 to 0.09375
Outputs:
- block_output: bfloat16 [288, 2304], P('groups', ('latent', 'hidden')), parts along dimension 0
- dictionary_grad: bfloat16 [8192, 4608], P(('latent', 'hidden'), 'groups'), parts along dimension 1
There are 2 independent parts, one for each index of `groups`. A program takes and returns all parts, laid end to end along the dimension named above; an argument that names none is the same for every part. Nothing has to cross between parts.
Inputs may be any that keep to these rules, and one draw needn't show every extreme that they name: `dictionary`: every entry is a whole multiple of 2^-10, at most 119 such units in magnitude. `encoder_bias`: every entry is a whole multiple of 2^-16.
All inputs are finite; a program needn't handle non-finite values.
Results may differ from a plain program's by a relative error of at most 0.0072.
Values may be sent and summed in bfloat16 or wider, within the bound.
A program may use at most 64 MiB of HBM per device.

v0:
```python
import types

import jax
import jax.numpy as jnp
from jax import lax
from jax.experimental import pallas as pl
from jax.experimental.pallas import tpu as pltpu
from jax.sharding import PartitionSpec as P

ROWS = 8
LANES = 128
TILE = 256
MESH = pl.DeviceIdType.MESH
F32 = jnp.float32
BF16 = jnp.bfloat16


def group_kernel(L, H, refs_in, refs_out, s):
    (codes_x, codes_u, dic_hbm, ebias, dbias, gain, gate_hbm, up_hbm, down_hbm) = refs_in
    (out_cols, out_left, out_right) = refs_out
    me = lax.axis_index("latent")
    h = lax.axis_index("hidden")
    other = 1 - h
    rows, own_width = codes_x.shape
    width = dic_hbm.shape[1]
    units = dic_hbm.shape[0]
    C = rows // ROWS
    K = C // H
    extra = K - L
    n_dev = L * H
    mine = me * H + h
    pad = s.stage_x.shape[2]

    def ext(hid):
        return (2 + 3 * hid) % L

    def at(lat, hid):
        return {"latent": lat, "hidden": hid}

    def rcopy(src, dst, ss, rs, lat, hid):
        return pltpu.make_async_remote_copy(
            src_ref=src, dst_ref=dst, send_sem=ss, recv_sem=rs,
            device_id=at(lat, hid), device_id_type=MESH,
        )

    def each(n, body):
        def step(i, carry):
            body(i)
            return carry

        lax.fori_loop(0, n, step, 0)

    def slots(body):
        body(0, me)
        if extra:
            @pl.when(me == ext(h))
            def _():
                body(1, L)

    loads = []
    for i, (src, dst) in enumerate(
        ((dic_hbm, s.dic), (down_hbm, s.down), (gate_hbm, s.gate), (up_hbm, s.up))
    ):
        cp = pltpu.make_async_copy(src, dst, s.load_sem.at[i])
        cp.start()
        loads.append(cp)

    barrier = pltpu.get_barrier_semaphore()

    def greet(j):
        pl.semaphore_signal(barrier, inc=1, device_id=at(lax.rem(me + j, L), other), device_id_type=MESH)

        @pl.when(j > 0)
        def _():
            pl.semaphore_signal(barrier, inc=1, device_id=at(lax.rem(me + j, L), h), device_id_type=MESH)

    each(L, greet)

    def stage(codes, buf):
        value = codes[...].astype(F32) * (2.0 ** (-6))
        value = jnp.concatenate([value, jnp.zeros((rows, pad - own_width), F32)], axis=1)
        buf[...] = value.reshape(C, ROWS, pad).astype(BF16)

    stage(codes_x, s.stage_x)
    stage(codes_u, s.stage_u)
    pl.semaphore_wait(barrier, n_dev - 1)

    def turn_start(buf, arr, ss, rs):
        def one(j):
            lat = lax.rem(me + j, L)
            for hid in range(H):
                c = hid * K + lat
                same = jnp.logical_and(lat == me, h == hid)

                @pl.when(jnp.logical_not(same))
                def _():
                    rcopy(buf.at[c], arr.at[0, mine], ss.at[c], rs.at[0, mine], lat, hid).start()

                @pl.when(same)
                def _():
                    arr[0, mine] = buf[c]

        each(L, one)
        if extra:
            for hid in range(H):
                c = hid * K + L
                same = jnp.logical_and(ext(hid) == me, h == hid)

                @pl.when(jnp.logical_not(same))
                def _():
                    rcopy(buf.at[c], arr.at[1, mine], ss.at[c], rs.at[1, mine], ext(hid), hid).start()

                @pl.when(same)
                def _():
                    arr[1, mine] = buf[c]

    def turn_finish(arr, rs, full):
        def one(slot, k):
            def get(i):
                @pl.when(i != mine)
                def _():
                    rcopy(arr.at[slot, i], arr.at[slot, i], rs.at[slot, i], rs.at[slot, i], me, other).wait_recv()

            each(n_dev, get)
            pieces = [arr[slot, i].astype(F32)[:, :own_width] for i in range(n_dev)]
            full[h * K + k] = jnp.concatenate(pieces, axis=1).astype(BF16)

        slots(one)

    def turn_drain(buf, ss):
        def one(j):
            lat = lax.rem(me + j, L)
            for hid in range(H):
                c = hid * K + lat

                @pl.when(jnp.logical_not(jnp.logical_and(lat == me, h == hid)))
                def _():
                    rcopy(buf.at[c], buf.at[c], ss.at[c], ss.at[c], lat, hid).wait_send()

        each(L, one)
        if extra:
            for hid in range(H):
                c = hid * K + L

                @pl.when(jnp.logical_not(jnp.logical_and(ext(hid) == me, h == hid)))
                def _():
                    rcopy(buf.at[c], buf.at[c], ss.at[c], ss.at[c], ext(hid), hid).wait_send()

    X = 2
    Z = L // X
    z, x = me // X, lax.rem(me, X)
    across_me = z * X + 1 - x

    def peer(j):
        if Z == 4:
            return (z + 1 - 2 * lax.rem(z, 2), z + 2 - 4 * (z // 2), 3 - z)[j]
        return lax.rem(z + 1 + j, Z)

    def in_column(j):
        return peer(j) * X + x

    def beside(j):
        return peer(j) * X + 1 - x

    near = range(Z - 1)
    far = (1, 2, 0) if Z == 4 else near
    ext_here = lax.rem(ext(h), X) == x
    ext_mine = me == ext(h)
    ext_passes = jnp.logical_and(ext_here, jnp.logical_not(ext_mine))

    def when_extra(cond, body):
        if extra:
            @pl.when(cond)
            def _():
                body(L)

    def wait_here(buf, sem):
        rcopy(buf, buf, sem, sem, me, other).wait_recv()

    def wait_sent(buf, sem):
        rcopy(buf, buf, sem, sem, me, other).wait_send()

    def hand_over(full, a, k):
        c = h * K + k
        rcopy(full.at[c], full.at[c], s.ag_fs.at[a, k], s.ag_fr.at[a, k], me, other).start()

    def step_across(full, a, k):
        c = h * K + k
        rcopy(full.at[c], full.at[c], s.ag_xs.at[a, k], s.ag_xr.at[a, k], across_me, h).start()

    def spread_start(full, a):
        def one(slot, k):
            c = h * K + k
            for j in far:
                rcopy(full.at[c], full.at[c], s.ag_ss.at[a, slot, j], s.ag_rr.at[a, k], in_column(j), h).start()
            step_across(full, a, k)
            hand_over(full, a, k)

        slots(one)

    def relay_column(full, a, k):
        wait_here(full.at[h * K + k], s.ag_rr.at[a, k])
        step_across(full, a, k)
        hand_over(full, a, k)

    def relay_across(full, a, k):
        wait_here(full.at[h * K + k], s.ag_xr.at[a, k])
        hand_over(full, a, k)

    def spread_column(full, a):
        for j in near:
            relay_column(full, a, in_column(j))
        when_extra(ext_passes, lambda k: relay_column(full, a, k))

    def spread_across(full, a):
        relay_across(full, a, across_me)
        for j in near:
            relay_across(full, a, beside(j))
        when_extra(jnp.logical_not(ext_here), lambda k: relay_across(full, a, k))

    def spread_take(full, a):
        each(K, lambda k: wait_here(full.at[other * K + k], s.ag_fr.at[a, k]))

    def spread_drain(full, a):
        def one(slot, k):
            for j in near:
                wait_sent(full.at[h * K + k], s.ag_ss.at[a, slot, j])

        slots(one)
        each(Z, lambda zz: wait_sent(full.at[h * K + zz * X + x], s.ag_xs.at[a, zz * X + x]))
        when_extra(ext_here, lambda k: wait_sent(full.at[h * K + k], s.ag_xs.at[a, k]))
        each(K, lambda k: wait_sent(full.at[h * K + k], s.ag_fs.at[a, k]))

    def rows_of(full, dst):
        dst[...] = full[...].astype(F32).reshape(rows, width).astype(BF16)

    def span(t, size):
        return pl.ds(pl.multiple_of(t * size, size), size)

    wide = 3 * TILE if width % (3 * TILE) == 0 else LANES
    def sum_tile(a, t, value):
        cols = span(t, wide)
        s.own[a, :, :, cols] = value.reshape(C, ROWS, wide)
        rcopy(
            s.own.at[a, pl.ds(other * K, K), :, cols], s.sib.at[a, :, :, cols],
            s.rs_cs.at[a, t], s.rs_cr.at[a, t], me, other,
        ).start()

    def sum_start(a):
        each(width // wide, lambda t: wait_here(s.sib.at[a, :, :, span(t, wide)], s.rs_cr.at[a, t]))

    def sum_chip(a, k):
        return s.own[a, h * K + k] + s.sib[a, k]

    def sum_middle(a):
        def leave(k):
            s.comb[a, k] = sum_chip(a, k).astype(BF16)
            rcopy(s.comb.at[a, k], s.xbuf.at[a, k], s.rs_xs.at[a, k], s.rs_xr.at[a, k], across_me, h).start()

        for j in far:
            leave(beside(j))
        when_extra(jnp.logical_not(ext_here), leave)
        leave(across_me)

    def sum_cross(a):
        def total(k):
            value = sum_chip(a, k)
            wait_here(s.xbuf.at[a, k], s.rs_xr.at[a, k])
            return value + s.xbuf[a, k].astype(F32)

        def leave(slot, k, owner):
            s.comb[a, k] = total(k).astype(BF16)
            rcopy(s.comb.at[a, k], s.rbuf.at[a, slot, z], s.rs_ss.at[a, k], s.rs_rr.at[a, slot, z], owner, h).start()

        for j in far:
            leave(0, in_column(j), in_column(j))
        when_extra(ext_passes, lambda k: leave(1, k, ext(h)))
        s.acc[a, 0] = total(me)

        def keep(k):
            s.acc[a, 1] = total(k)

        when_extra(ext_mine, keep)

    def sum_value(a, slot):
        value = s.acc[a, slot]
        for j in near:
            wait_here(s.rbuf.at[a, slot, peer(j)], s.rs_rr.at[a, slot, peer(j)])
            value = value + s.rbuf[a, slot, peer(j)].astype(F32)
        return value

    def sum_drain(a):
        each(width // wide, lambda t: wait_sent(s.sib.at[a, :, :, span(t, wide)], s.rs_cs.at[a, t]))
        each(Z, lambda zz: wait_sent(s.xbuf.at[a, zz * X + 1 - x], s.rs_xs.at[a, zz * X + 1 - x]))
        when_extra(jnp.logical_not(ext_here), lambda k: wait_sent(s.xbuf.at[a, k], s.rs_xs.at[a, k]))
        for j in near:
            wait_sent(s.xbuf.at[a, in_column(j)], s.rs_ss.at[a, in_column(j)])
        when_extra(ext_passes, lambda k: wait_sent(s.xbuf.at[a, k], s.rs_ss.at[a, k]))

    across = (((1,), (1,)), ((), ()))

    def mm_t(x, w):
        return lax.dot_general(x, w, across, preferred_element_type=F32)

    def mm(x, w):
        return lax.dot_general(x, w, (((1,), (0,)), ((), ())), preferred_element_type=F32)

    deep = TILE if units % TILE == 0 else units
    n_deep = units // deep

    turn_start(s.stage_x, s.arr_x, s.tx_ss.at[0], s.tx_rs.at[0])
    turn_start(s.stage_u, s.arr_u, s.tx_ss.at[1], s.tx_rs.at[1])
    turn_finish(s.arr_x, s.tx_rs.at[0], s.full_x)
    spread_start(s.full_x, 0)
    turn_finish(s.arr_u, s.tx_rs.at[1], s.full_u)
    spread_column(s.full_x, 0)
    spread_start(s.full_u, 1)
    spread_across(s.full_x, 0)
    spread_take(s.full_x, 0)
    rows_of(s.full_x, s.both_in.at[pl.ds(rows, rows)])
    x_rows = s.both_in.at[pl.ds(rows, rows)]

    def store_right(part):
        at_rows = pl.ds(part * rows, rows)
        return pltpu.make_async_copy(s.both_in.at[at_rows], out_right.at[at_rows], s.out_sem.at[part])

    store_right(1).start()
    loads[0].wait()
    for t in range(n_deep):
        cols = pl.ds(t * deep, deep)
        pre = mm_t(x_rows[...], s.dic[cols, :]) + ebias[:, cols]
        s.pre[:, cols] = pre
        s.lat[:, cols] = jnp.maximum(pre, 0.0).astype(BF16)
    spread_column(s.full_u, 1)
    each(width // wide, lambda t: sum_tile(0, t, mm(s.lat[...], s.dic[:, span(t, wide)])))
    sum_start(0)
    sum_middle(0)
    spread_across(s.full_u, 1)
    sum_cross(0)
    spread_take(s.full_u, 1)
    rows_of(s.full_u, s.u_rows)
    loads[1].wait()
    for t in range(n_deep):
        cols = pl.ds(t * deep, deep)
        s.hgrad[:, cols] = mm_t(s.u_rows[...], s.down[cols, :])

    def norm(slot, k):
        rebuilt = sum_value(0, slot) + dbias[...]
        inverse = lax.rsqrt(jnp.sum(rebuilt * rebuilt, axis=1, keepdims=True) / width + 1e-06)
        s.rebuilt[slot] = rebuilt
        s.inverse[slot] = jnp.broadcast_to(inverse, (ROWS, LANES))
        s.full_n[h * K + k] = (rebuilt * inverse * gain[...]).astype(BF16)

    slots(norm)
    spread_start(s.full_n, 2)
    s.lat_t[:, :rows] = jnp.maximum(s.pre[...], 0.0).T.astype(BF16)
    spread_column(s.full_n, 2)
    spread_across(s.full_n, 2)
    spread_take(s.full_n, 2)
    rows_of(s.full_n, s.n_rows)
    loads[2].wait()
    loads[3].wait()
    for t in range(n_deep):
        cols = pl.ds(t * deep, deep)
        g = mm_t(s.n_rows[...], s.gate[cols, :])
        u = mm_t(s.n_rows[...], s.up[cols, :])
        th = jnp.tanh(0.7978845608028654 * (g + 0.044715 * g * g * g))
        value = 0.5 * g * (1.0 + th)
        slope = 0.5 * (1.0 + th) + 0.5 * g * (1.0 - th * th) * 0.7978845608028654 * (
            1.0 + 3.0 * 0.044715 * g * g
        )
        hg = s.hgrad[:, cols]
        s.hid[:, cols] = (value * u).astype(BF16)
        s.ggrad[:, cols] = (hg * u * slope).astype(BF16)
        s.ugrad[:, cols] = (hg * value).astype(BF16)
    each(
        width // wide,
        lambda t: sum_tile(
            1,
            t,
            mm(s.ggrad[...], s.gate[:, span(t, wide)]) + mm(s.ugrad[...], s.up[:, span(t, wide)]),
        ),
    )
    sum_start(1)
    sum_middle(1)
    each(width // wide, lambda t: sum_tile(2, t, mm(s.hid[...], s.down[:, span(t, wide)])))
    sum_start(2)
    sum_cross(1)
    sum_middle(2)
    sum_cross(2)

    def back(slot, k):
        scaled = sum_value(1, slot) * gain[...]
        rebuilt = s.rebuilt[slot]
        inverse = s.inverse[slot][:, :1]
        inner = jnp.sum(scaled * rebuilt, axis=1, keepdims=True)
        target = s.full_x[h * K + k].astype(F32)
        s.full_r[h * K + k] = (
            inverse * scaled - inverse * inverse * inverse * rebuilt * (inner / width) + (rebuilt - target)
        ).astype(BF16)

    def turn_back(slot, k):
        value = sum_value(2, slot)
        c = h * K + k
        for i in range(n_dev):
            piece = value[:, i * own_width : (i + 1) * own_width]
            piece = jnp.concatenate([piece, jnp.zeros((ROWS, pad - own_width), F32)], axis=1)
            s.stage_o[slot, i] = piece.astype(BF16)

        def send(i):
            @pl.when(i != mine)
            def _():
                rcopy(s.stage_o.at[slot, i], s.arr_o.at[c], s.to_ss.at[slot, i], s.to_rs.at[c], i // H, lax.rem(i, H)).start()

            @pl.when(i == mine)
            def _():
                s.arr_o[c] = s.stage_o[slot, i]

        each(n_dev, send)

    slots(back)
    spread_start(s.full_r, 3)
    spread_column(s.full_r, 3)
    spread_across(s.full_r, 3)
    slots(turn_back)
    spread_take(s.full_r, 3)
    rows_of(s.full_r, s.both_in.at[pl.ds(0, rows)])
    r_rows = s.both_in.at[pl.ds(0, rows)]
    store_right(0).start()
    for t in range(n_deep):
        cols = pl.ds(t * deep, deep)
        grad = mm_t(r_rows[...], s.dic[cols, :])
        grad = jnp.where(s.pre[:, cols] > 0.0, grad, 0.0)
        s.lat_t[cols, rows:] = grad.T.astype(BF16)

    store_left = pltpu.make_async_copy(s.lat_t, out_left, s.out_sem.at[2])
    store_left.start()

    def got(k):
        for hid in range(H):
            c = hid * K + k
            is_mine = jnp.logical_and(h == hid, (ext(hid) if k is L else k) == me)

            @pl.when(jnp.logical_not(is_mine))
            def _():
                rcopy(s.arr_o.at[c], s.arr_o.at[c], s.to_rs.at[c], s.to_rs.at[c], me, other).wait_recv()

    each(L, got)
    if extra:
        got(L)
    out_cols[...] = s.arr_o[...]

    turn_drain(s.stage_x, s.tx_ss.at[0])
    turn_drain(s.stage_u, s.tx_ss.at[1])
    for a, full in enumerate((s.full_x, s.full_u, s.full_n, s.full_r)):
        spread_drain(full, a)
    for a in range(3):
        sum_drain(a)

    def out_gone(slot, k):
        def one(i):
            @pl.when(i != mine)
            def _():
                rcopy(s.stage_o.at[slot, i], s.stage_o.at[slot, i], s.to_ss.at[slot, i], s.to_ss.at[slot, i], me, other).wait_send()

        each(n_dev, one)

    slots(out_gone)
    store_left.wait()
    for part in (0, 1):
        store_right(part).wait()


def run_group(L, H, *args):
    codes, dic = args[0], args[2]
    rows, own_width = codes.shape
    units, width = dic.shape
    C = rows // ROWS
    K = C // H
    n_dev = L * H
    pad = -(-own_width // LANES) * LANES
    wide = 3 * TILE if width % (3 * TILE) == 0 else LANES
    V, D, R = pltpu.VMEM, pltpu.SemaphoreType.DMA, ROWS
    scratch = dict(
        dic=V((units, width), BF16), gate=V((units, width), BF16),
        up=V((units, width), BF16), down=V((units, width), BF16),
        stage_x=V((C, R, pad), BF16), stage_u=V((C, R, pad), BF16),
        arr_x=V((2, n_dev, R, pad), BF16), arr_u=V((2, n_dev, R, pad), BF16),
        full_x=V((C, R, width), BF16), full_u=V((C, R, width), BF16),
        full_n=V((C, R, width), BF16), full_r=V((C, R, width), BF16),
        both_in=V((2 * rows, width), BF16), u_rows=V((rows, width), BF16), n_rows=V((rows, width), BF16),
        pre=V((rows, units), F32), hgrad=V((rows, units), F32),
        lat=V((rows, units), BF16), hid=V((rows, units), BF16),
        ggrad=V((rows, units), BF16), ugrad=V((rows, units), BF16),
        lat_t=V((units, 2 * rows), BF16),
        own=V((3, C, R, width), F32), xbuf=V((3, K, R, width), BF16),
        sib=V((3, K, R, width), F32), comb=V((3, K, R, width), BF16),
        rbuf=V((3, 2, L // 2, R, width), BF16), acc=V((3, 2, R, width), F32),
        rebuilt=V((2, R, width), F32), inverse=V((2, R, LANES), F32),
        stage_o=V((2, n_dev, R, pad), BF16), arr_o=V((C, R, pad), BF16),
        load_sem=D((4,)), out_sem=D((3,)),
        tx_ss=D((2, C)), tx_rs=D((2, 2, n_dev)),
        ag_ss=D((4, 2, L // 2)), ag_xs=D((4, K)), ag_xr=D((4, K)), ag_rr=D((4, K)), ag_fs=D((4, K)), ag_fr=D((4, K)),
        rs_cs=D((3, width // wide)), rs_cr=D((3, width // wide)), rs_ss=D((3, K)), rs_rr=D((3, 2, L // 2)), rs_xs=D((3, K)), rs_xr=D((3, K)),
        to_ss=D((2, n_dev)), to_rs=D((C,)),
    )
    names = list(scratch)

    def body(*refs):
        group_kernel(L, H, refs[:9], refs[9:12], types.SimpleNamespace(**dict(zip(names, refs[12:]))))

    any_spec = pl.BlockSpec(memory_space=pl.ANY)
    vm = pl.BlockSpec(memory_space=pltpu.VMEM)
    cols, left, right = pl.pallas_call(
        body,
        name="group_step",
        out_shape=(
            jax.ShapeDtypeStruct((C, R, pad), BF16),
            jax.ShapeDtypeStruct((units, 2 * rows), BF16),
            jax.ShapeDtypeStruct((2 * rows, width), BF16),
        ),
        in_specs=[vm, vm, any_spec, vm, vm, vm, any_spec, any_spec, any_spec],
        out_specs=(vm, any_spec, any_spec),
        scratch_shapes=[scratch[n] for n in names],
        compiler_params=pltpu.CompilerParams(collective_id=0, has_side_effects=True, vmem_limit_bytes=60 * 2**20),
    )(*args)

    def product(cols, left, right, block, grad):
        grad[...] = jnp.dot(left[...], right[...], preferred_element_type=F32).astype(BF16)

        @pl.when(pl.program_id(0) == 0)
        def _():
            block[...] = cols[...].astype(F32).reshape(rows, pad)[:, :own_width].astype(BF16)

    step = width // 3 if width % (3 * LANES) == 0 else wide
    return pl.pallas_call(
        product,
        name="dictionary_product",
        grid=(width // step,),
        out_shape=(
            jax.ShapeDtypeStruct((rows, own_width), BF16),
            jax.ShapeDtypeStruct((units, width), BF16),
        ),
        in_specs=[
            pl.BlockSpec((C, R, pad), lambda t: (0, 0, 0)),
            pl.BlockSpec((units, 2 * rows), lambda t: (0, 0)),
            pl.BlockSpec((2 * rows, step), lambda t: (0, t)),
        ],
        out_specs=(
            pl.BlockSpec((rows, own_width), lambda t: (0, 0)),
            pl.BlockSpec((units, step), lambda t: (0, t)),
        ),
    )(cols, left, right)


def fits(L, H, rows, width, units, units_mlp):
    if H != 2 or rows % (ROWS * H) or width % LANES or units % LANES or units != units_mlp:
        return False
    return L >= 6 and L % 2 == 0 and 0 <= rows // ROWS // H - L <= 1


CODE_STEP = 2.0 ** (-6)
NORM_EPSILON = 1e-06
GELU_ROOT = 0.7978845608028654
GELU_CUBIC = 0.044715
ACROSS = (((1,), (1,)), ((), ()))
DOWNWARD = (((0,), (0,)), ((), ()))


def gelu_parts(values):
    argument = GELU_ROOT * (values + GELU_CUBIC * values * values * values)
    tanh_value = jnp.tanh(argument)
    result = 0.5 * values * (1.0 + tanh_value)
    derivative = 0.5 * (1.0 + tanh_value) + 0.5 * values * (
        1.0 - tanh_value * tanh_value
    ) * GELU_ROOT * (1.0 + 3.0 * GELU_CUBIC * values * values)
    return (result, derivative)


def per_device(
    input_codes,
    cotangent_codes,
    dictionary,
    encoder_bias,
    decoder_bias,
    norm_gain,
    gate_weight,
    up_weight,
    down_weight,
):
    L, H = lax.axis_size("latent"), lax.axis_size("hidden")
    rows, width = input_codes.shape[0], dictionary.shape[1]
    if fits(L, H, rows, width, dictionary.shape[0], gate_weight.shape[0]):
        return run_group(
            L, H, input_codes, cotangent_codes, dictionary, encoder_bias[None, :], decoder_bias,
            norm_gain, gate_weight, up_weight, down_weight,
        )
    own_width = input_codes.shape[1]
    model_width = own_width * lax.axis_size(("latent", "hidden"))
    cotangent_local = (cotangent_codes.astype(jnp.float32) * CODE_STEP).astype(jnp.bfloat16)
    hidden_grad = None
    inputs_local = (input_codes.astype(jnp.float32) * CODE_STEP).astype(jnp.bfloat16)
    inputs = lax.all_gather(inputs_local, ("latent", "hidden"), axis=1, tiled=True)
    preact = (
        lax.dot_general(inputs, dictionary, ACROSS, preferred_element_type=jnp.float32)
        + encoder_bias
    )
    latents = jnp.maximum(preact, 0.0).astype(jnp.bfloat16)
    partial_value = jnp.dot(latents, dictionary, preferred_element_type=jnp.float32)
    rebuilt = lax.psum(partial_value, ("latent", "hidden")) + decoder_bias
    inverse = lax.rsqrt(
        jnp.sum(rebuilt * rebuilt, axis=1, keepdims=True) / model_width + NORM_EPSILON
    )
    normed = (rebuilt * inverse * norm_gain).astype(jnp.bfloat16)
    target = inputs.astype(jnp.float32)
    gate_proj = lax.dot_general(normed, gate_weight, ACROSS, preferred_element_type=jnp.float32)
    up_proj = lax.dot_general(normed, up_weight, ACROSS, preferred_element_type=jnp.float32)
    gelu_value, gelu_slope = gelu_parts(gate_proj)
    hidden = (gelu_value * up_proj).astype(jnp.bfloat16)
    output_terms = jnp.dot(hidden, down_weight, preferred_element_type=jnp.float32)
    block_output = lax.psum_scatter(
        output_terms, ("latent", "hidden"), scatter_dimension=1, tiled=True
    ).astype(jnp.bfloat16)
    hidden_grad = lax.dot_general(
        lax.all_gather(cotangent_local, ("latent", "hidden"), axis=1, tiled=True),
        down_weight,
        ACROSS,
        preferred_element_type=jnp.float32,
    )
    gate_grad = (hidden_grad * up_proj * gelu_slope).astype(jnp.bfloat16)
    up_grad = (hidden_grad * gelu_value).astype(jnp.bfloat16)
    partial_grad = jnp.dot(gate_grad, gate_weight, preferred_element_type=jnp.float32) + jnp.dot(
        up_grad, up_weight, preferred_element_type=jnp.float32
    )
    scaled = lax.psum(partial_grad, ("latent", "hidden")) * norm_gain
    inner_row = jnp.sum(scaled * rebuilt, axis=1, keepdims=True)
    inverse_cube = inverse * inverse * inverse
    rebuilt_grad = (
        inverse * scaled - inverse_cube * rebuilt * (inner_row / model_width) + (rebuilt - target)
    ).astype(jnp.bfloat16)
    latent_grad = lax.dot_general(
        rebuilt_grad, dictionary, ACROSS, preferred_element_type=jnp.float32
    )
    preact_grad = jnp.where(preact > 0.0, latent_grad, 0.0).astype(jnp.bfloat16)
    dictionary_grad = lax.dot_general(
        latents, rebuilt_grad, DOWNWARD, preferred_element_type=jnp.float32
    ) + lax.dot_general(preact_grad, inputs, DOWNWARD, preferred_element_type=jnp.float32)
    return (block_output, dictionary_grad.astype(jnp.bfloat16))


def solution(mesh):
    in_specs = (
        P("groups", ("latent", "hidden")),
        P("groups", ("latent", "hidden")),
        P(("latent", "hidden"), None),
        P(("latent", "hidden")),
        P(),
        P(),
        P(("latent", "hidden"), None),
        P(("latent", "hidden"), None),
        P(("latent", "hidden"), None),
    )
    out_specs = (P("groups", ("latent", "hidden")), P(("latent", "hidden"), "groups"))
    return jax.shard_map(
        per_device, mesh=mesh, in_specs=in_specs, out_specs=out_specs, check_vma=False
    )
```

profile of v0, /device:TPU:0, one launch (start us, length us, event | category | flops | bytes accessed | tf_op | source)
XLA Modules:
  0.0 79.9 jit_solution(17865088838138463439)
XLA Ops:
  0.6 74.8 %group_step.1 = (bf16[18,8,256]{2,1,0:T(8,128)(2,1)}, bf16[512,288]{1,0:T(8,128)(2,1)}, bf16[288,2304]{1,0:T(8,128)(2,1)}) custom-call(s32[144,144]{1,0:T(8,128)} %refs_0_.1, s32[144,144]{1,0:T(8,128)} %refs_1_.1, bf16[512,2304]{1,0:T(8,128)(2,1)} %refs_2_.1, f32[1,512]{1,0:T(1,128)} %bitcast.1, f32[2304]{0:T(1024)} %refs_4_.1, f32[2304]{0:T(1024)} %refs_5_.1, ...), custom_call_target="tpu_custom_call" | custom-call | tf_op jit(solution)/shard_map/group_step/pallas_call | solution.py:514
  75.4 4.5 %dictionary_product.1 = (bf16[144,144]{1,0:T(8,128)(2,1)}, bf16[512,2304]{1,0:T(8,128)(2,1)}) custom-call(bf16[18,8,256]{2,1,0:T(8,128)(2,1)} %get-tuple-element.5.cols, bf16[512,288]{1,0:T(8,128)(2,1)} %get-tuple-element.6.left, bf16[288,2304]{1,0:T(8,128)(2,1)} %get-tuple-element.7.right), custom_call_target="tpu_custom_call" | custom-call | tf_op jit(solution)/shard_map/dictionary_product/pallas_call | solution.py:536
where the time goes:
time: 80.1 us; the launch traced here: 79.9 us
  Pallas kernels  79.3 us (99%)
    pallas_call x1, Pallas kernels, run_group(): pl.pallas_call(body, name='group_step', out_shape=(jax.ShapeDtypeStruct((...  74.8 us
    pallas_call x1, Pallas kernels, run_group(): pl.pallas_call(product, name='dictionary_product', grid=(width // step,),...  4.51 us

commit v1 on v0

v1 whole, which is shorter than its diff:
```python
import types

import jax
import jax.numpy as jnp
from jax import lax
from jax.experimental import pallas as pl
from jax.experimental.pallas import tpu as pltpu
from jax.sharding import PartitionSpec as P

ROWS = 8
PACK = 16
LANES = 128
TILE = 256
MESH = pl.DeviceIdType.MESH
F32 = jnp.float32
BF16 = jnp.bfloat16


def group_kernel(L, H, refs_in, refs_out, s):
    (codes_x, codes_u, dic_hbm, ebias_in, dbias_in, gain_in, gate_hbm, up_hbm, down_hbm) = refs_in
    (out_cols, left, right) = refs_out
    me = lax.axis_index("latent")
    h = lax.axis_index("hidden")
    other = 1 - h
    rows, own_width = codes_x.shape
    width = dic_hbm.shape[1]
    units = dic_hbm.shape[0]
    C = rows // ROWS
    K = C // H
    extra = K - L
    n_dev = L * H
    mine = me * H + h
    pad = out_cols.shape[2]
    rest = own_width - LANES
    per = LANES // rest

    def ext(hid):
        return (2 + 3 * hid) % L

    def at(lat, hid):
        return {"latent": lat, "hidden": hid}

    def rcopy(src, dst, ss, rs, lat, hid):
        return pltpu.make_async_remote_copy(
            src_ref=src, dst_ref=dst, send_sem=ss, recv_sem=rs,
            device_id=at(lat, hid), device_id_type=MESH,
        )

    def each(n, body):
        def step(i, carry):
            body(i)
            return carry

        lax.fori_loop(0, n, step, 0)

    def slots(body):
        body(0, me)
        if extra:
            @pl.when(me == ext(h))
            def _():
                body(1, L)

    barrier = pltpu.get_barrier_semaphore()
    for j in range(L):
        for i in range(H):
            if i or j:
                pl.semaphore_signal(
                    barrier, inc=1, device_id=at(lax.rem(me + j, L), lax.rem(h + i, H)), device_id_type=MESH
                )

    loads = []
    for i, (src, dst) in enumerate((
        (codes_x, s.codes_x), (codes_u, s.codes_u), (dic_hbm, s.dic), (ebias_in, s.ebias),
        (dbias_in, s.dbias), (gain_in, s.gain), (down_hbm, s.down), (gate_hbm, s.gate), (up_hbm, s.up),
    )):
        cp = pltpu.make_async_copy(src, dst, s.load_sem.at[i])
        cp.start()
        loads.append(cp)

    def stage(codes, arr):
        value = codes[...].astype(F32) * (2.0 ** (-6))
        shift = lax.rem(mine * own_width, LANES)
        arr[mine, pl.ds(0, rows)] = pltpu.roll(value[:, :LANES], shift, 1).astype(BF16)
        over = jnp.concatenate([value[:, LANES:], jnp.zeros((rows, LANES - rest), F32)], axis=1)
        for b in range(s.gx.shape[1] // PACK - rows // PACK):
            packed = None
            for g in range(b * per, min((b + 1) * per, rows // PACK)):
                part = over[g * PACK : (g + 1) * PACK]
                part = pltpu.roll(part, (g % per) * rest, 1) if g % per else part
                packed = part if packed is None else packed + part
            arr[mine, pl.ds(rows + b * PACK, PACK)] = packed.astype(BF16)

    X = 2
    Z = L // X
    z, x = me // X, lax.rem(me, X)
    across_me = z * X + 1 - x

    def peer(j):
        if Z == 4:
            return (z + 1 - 2 * lax.rem(z, 2), z + 2 - 4 * (z // 2), 3 - z)[j]
        return lax.rem(z + 1 + j, Z)

    def in_column(j):
        return peer(j) * X + x

    def beside(j):
        return peer(j) * X + 1 - x

    near = range(Z - 1)
    far = (1, 2, 0) if Z == 4 else near
    ext_here = lax.rem(ext(h), X) == x
    ext_mine = me == ext(h)
    ext_passes = jnp.logical_and(ext_here, jnp.logical_not(ext_mine))

    def when_extra(cond, body):
        if extra:
            @pl.when(cond)
            def _():
                body(L, Z)

    def wait_here(buf, sem):
        rcopy(buf, buf, sem, sem, me, other).wait_recv()

    def wait_sent(buf, sem):
        rcopy(buf, buf, sem, sem, me, other).wait_send()

    def cols_start(arr, a):
        for j in far:
            for lat in (beside(j), in_column(j)):
                rcopy(arr.at[mine], arr.at[mine], s.col_ss.at[a], s.col_rs.at[a, me], lat, h).start()
        rcopy(arr.at[mine], arr.at[mine], s.col_ss.at[a], s.col_rs.at[a, me], across_me, h).start()
        rcopy(arr.at[mine], arr.at[mine], s.col_fs.at[a], s.col_fr.at[a], me, other).start()

    def cols_relay(arr, a):
        order = [across_me]
        for j in near:
            order += [in_column(j), beside(j)]
        for lat in order:
            piece = arr.at[lat * H + h]
            wait_here(piece, s.col_rs.at[a, lat])
            rcopy(piece, piece, s.col_fs.at[a], s.col_fr.at[a], me, other).start()

    def cols_take(arr, a):
        wait_here(arr.at[pl.ds(0, L)], s.col_fr.at[a])

    def cols_drain(arr, a):
        wait_sent(arr.at[pl.ds(0, L - 1)], s.col_ss.at[a])
        wait_sent(arr.at[pl.ds(0, L)], s.col_fs.at[a])

    def cols_rows(arr, put):
        lane = lax.broadcasted_iota(jnp.int32, (rows, LANES), 1)

        def main(i):
            return arr[i, pl.ds(0, rows)].astype(F32)

        def over(i):
            block = arr[i, pl.ds(rows, s.gx.shape[1] - rows)].astype(F32)
            parts = []
            for g in range(rows // PACK):
                b = g // per
                move = (i * own_width - (g % per) * rest) % LANES
                part = block[b * PACK : (b + 1) * PACK]
                parts.append(pltpu.roll(part, move, 1) if move else part)
            return jnp.concatenate(parts, axis=0)

        for t in range(width // LANES):
            value = None
            for i in range(n_dev):
                first, offset = divmod(i * own_width, LANES)
                if first == t:
                    new = main(i)
                    value = new if value is None else jnp.where(lane >= offset, new, value)
                elif first == t - 1:
                    value = over(i)
                    if offset:
                        value = jnp.where(lane >= offset, value, main(i))
            put(t, value)

    def hand_over(full, a, k):
        c = h * K + k
        rcopy(full.at[c], full.at[c], s.ag_fs.at[a], s.ag_fr.at[a], me, other).start()

    def step_across(full, a, k, i):
        c = h * K + k
        rcopy(full.at[c], full.at[c], s.ag_xs.at[a], s.ag_xr.at[a, i], across_me, h).start()

    def spread_start(full, a):
        def one(slot, k):
            c = h * K + k
            i = Z if slot else z
            for j in far:
                rcopy(full.at[c], full.at[c], s.ag_ss.at[a, slot], s.ag_rr.at[a, i], in_column(j), h).start()
            step_across(full, a, k, i)
            hand_over(full, a, k)

        slots(one)

    def relay_column(full, a, k, i):
        wait_here(full.at[h * K + k], s.ag_rr.at[a, i])
        step_across(full, a, k, i)
        hand_over(full, a, k)

    def relay_across(full, a, k, i):
        wait_here(full.at[h * K + k], s.ag_xr.at[a, i])
        hand_over(full, a, k)

    def spread_column(full, a):
        for j in near:
            relay_column(full, a, in_column(j), peer(j))
        when_extra(ext_passes, lambda k, i: relay_column(full, a, k, i))

    def spread_across(full, a):
        relay_across(full, a, across_me, z)
        for j in near:
            relay_across(full, a, beside(j), peer(j))
        when_extra(jnp.logical_not(ext_here), lambda k, i: relay_across(full, a, k, i))

    def spread_take(full, a):
        wait_here(full.at[pl.ds(other * K, K)], s.ag_fr.at[a])

    def either(cond, body, less, more):
        if extra:
            @pl.when(cond)
            def _():
                body(more)

            @pl.when(jnp.logical_not(cond))
            def _():
                body(less)
        else:
            body(less)

    def spread_drain(full, a):
        slots(lambda slot, k: wait_sent(full.at[pl.ds(0, Z - 1)], s.ag_ss.at[a, slot]))
        either(ext_here, lambda n: wait_sent(full.at[pl.ds(0, n)], s.ag_xs.at[a]), Z, Z + 1)
        wait_sent(full.at[pl.ds(0, K)], s.ag_fs.at[a])

    def rows_of(full, dst):
        dst[...] = full[...].astype(F32).reshape(rows, width).astype(BF16)

    def sum_tile(a, t, value):
        cols = pl.ds(t * wide, wide)
        s.own[a, :, :, cols] = value.reshape(C, ROWS, wide)
        rcopy(
            s.own.at[a, pl.ds(other * K, K), :, cols], s.sib.at[a, :, :, cols],
            s.rs_cs.at[a], s.rs_cr.at[a], me, other,
        ).start()

    wide = 3 * TILE if width % (3 * TILE) == 0 else LANES
    n_wide = width // wide

    def sum_start(a):
        wait_here(s.sib.at[a], s.rs_cr.at[a])

    def sum_chip(a, k):
        return s.own[a, h * K + k] + s.sib[a, k]

    def sum_middle(a):
        def leave(k, i):
            s.comb[a, k] = sum_chip(a, k).astype(BF16)
            rcopy(s.comb.at[a, k], s.xbuf.at[a, k], s.rs_xs.at[a], s.rs_xr.at[a, i], across_me, h).start()

        for j in far:
            leave(beside(j), peer(j))
        when_extra(jnp.logical_not(ext_here), leave)
        leave(across_me, z)

    def sum_cross(a):
        def total(k, i):
            value = sum_chip(a, k)
            wait_here(s.xbuf.at[a, k], s.rs_xr.at[a, i])
            return value + s.xbuf[a, k].astype(F32)

        def leave(slot, k, i, owner):
            s.comb[a, k] = total(k, i).astype(BF16)
            rcopy(s.comb.at[a, k], s.rbuf.at[a, slot, z], s.rs_ss.at[a], s.rs_rr.at[a, slot], owner, h).start()

        for j in far:
            leave(0, in_column(j), peer(j), in_column(j))
        when_extra(ext_passes, lambda k, i: leave(1, k, i, ext(h)))
        s.acc[a, 0] = total(me, z)

        def keep(k, i):
            s.acc[a, 1] = total(k, i)

        when_extra(ext_mine, keep)

    def sum_value(a, slot):
        value = s.acc[a, slot]
        wait_here(s.rbuf.at[a, slot, pl.ds(0, Z - 1)], s.rs_rr.at[a, slot])
        for j in near:
            value = value + s.rbuf[a, slot, peer(j)].astype(F32)
        return value

    def sum_drain(a):
        wait_sent(s.sib.at[a], s.rs_cs.at[a])
        either(jnp.logical_not(ext_here), lambda n: wait_sent(s.xbuf.at[a, pl.ds(0, n)], s.rs_xs.at[a]), Z, Z + 1)
        either(ext_passes, lambda n: wait_sent(s.xbuf.at[a, pl.ds(0, n)], s.rs_ss.at[a]), Z - 1, Z)

    across = (((1,), (1,)), ((), ()))

    def mm_t(x, w):
        return lax.dot_general(x, w, across, preferred_element_type=F32)

    def mm(x, w):
        return lax.dot_general(x, w, (((1,), (0,)), ((), ())), preferred_element_type=F32)

    deep = TILE if units % TILE == 0 else units
    n_deep = units // deep

    loads[0].wait()
    stage(s.codes_x, s.gx)
    pl.semaphore_wait(barrier, n_dev - 1)
    cols_start(s.gx, 0)
    loads[1].wait()
    stage(s.codes_u, s.gu)
    cols_relay(s.gx, 0)
    cols_start(s.gu, 1)
    cols_take(s.gx, 0)
    x_rows = right.at[pl.ds(rows, rows)]
    r_rows = right.at[pl.ds(0, rows)]

    def put_x(t, value):
        right[pl.ds(rows, rows), t * LANES : (t + 1) * LANES] = value.astype(BF16)
        s.full_x[:, :, t * LANES : (t + 1) * LANES] = value.reshape(C, ROWS, LANES).astype(BF16)

    cols_rows(s.gx, put_x)
    loads[2].wait()
    loads[3].wait()
    for t in range(n_deep):
        cols = pl.ds(t * deep, deep)
        pre = mm_t(x_rows[...], s.dic[cols, :]) + s.ebias[:, cols]
        s.pre[:, cols] = pre
        left[pl.ds(0, rows), cols] = jnp.maximum(pre, 0.0).astype(BF16)
    for t in range(n_wide):
        sum_tile(0, t, mm(left[pl.ds(0, rows), :], s.dic[:, t * wide : (t + 1) * wide]))
    cols_relay(s.gu, 1)
    sum_start(0)
    sum_middle(0)
    sum_cross(0)
    cols_take(s.gu, 1)

    def put_u(t, value):
        s.u_rows[:, t * LANES : (t + 1) * LANES] = value.astype(BF16)

    cols_rows(s.gu, put_u)
    loads[6].wait()
    for t in range(n_deep):
        cols = pl.ds(t * deep, deep)
        s.hgrad[:, cols] = mm_t(s.u_rows[...], s.down[cols, :])
    loads[4].wait()
    loads[5].wait()

    def norm(slot, k):
        rebuilt = sum_value(0, slot) + s.dbias[...]
        inverse = lax.rsqrt(jnp.sum(rebuilt * rebuilt, axis=1, keepdims=True) / width + 1e-06)
        s.rebuilt[slot] = rebuilt
        s.inverse[slot] = jnp.broadcast_to(inverse, (ROWS, LANES))
        s.full_n[h * K + k] = (rebuilt * inverse * s.gain[...]).astype(BF16)

    slots(norm)
    spread_start(s.full_n, 0)
    loads[7].wait()
    loads[8].wait()
    spread_column(s.full_n, 0)
    spread_across(s.full_n, 0)
    spread_take(s.full_n, 0)
    rows_of(s.full_n, s.n_rows)
    for t in range(n_deep):
        cols = pl.ds(t * deep, deep)
        g = mm_t(s.n_rows[...], s.gate[cols, :])
        u = mm_t(s.n_rows[...], s.up[cols, :])
        th = jnp.tanh(0.7978845608028654 * (g + 0.044715 * g * g * g))
        value = 0.5 * g * (1.0 + th)
        slope = 0.5 * (1.0 + th) + 0.5 * g * (1.0 - th * th) * 0.7978845608028654 * (
            1.0 + 3.0 * 0.044715 * g * g
        )
        hg = s.hgrad[:, cols]
        s.hid[:, cols] = (value * u).astype(BF16)
        s.ggrad[:, cols] = (hg * u * slope).astype(BF16)
        s.ugrad[:, cols] = (hg * value).astype(BF16)
    for t in range(n_wide):
        cols = slice(t * wide, (t + 1) * wide)
        sum_tile(1, t, mm(s.ggrad[...], s.gate[:, cols]) + mm(s.ugrad[...], s.up[:, cols]))
    sum_start(1)
    sum_middle(1)
    for t in range(n_wide):
        sum_tile(2, t, mm(s.hid[...], s.down[:, t * wide : (t + 1) * wide]))
    sum_start(2)
    sum_cross(1)
    sum_middle(2)
    sum_cross(2)

    def back(slot, k):
        scaled = sum_value(1, slot) * s.gain[...]
        rebuilt = s.rebuilt[slot]
        inverse = s.inverse[slot][:, :1]
        inner = jnp.sum(scaled * rebuilt, axis=1, keepdims=True)
        target = s.full_x[h * K + k].astype(F32)
        s.full_r[h * K + k] = (
            inverse * scaled - inverse * inverse * inverse * rebuilt * (inner / width) + (rebuilt - target)
        ).astype(BF16)

    def turn_back(slot, k):
        value = sum_value(2, slot)
        c = h * K + k
        for i in range(n_dev):
            piece = value[:, i * own_width : (i + 1) * own_width]
            piece = jnp.concatenate([piece, jnp.zeros((ROWS, pad - own_width), F32)], axis=1)
            s.stage_o[slot, i] = piece.astype(BF16)

        def send(i):
            @pl.when(i != mine)
            def _():
                rcopy(s.stage_o.at[slot, i], s.arr_o.at[c], s.to_ss.at[slot], s.to_rs.at[0], i // H, lax.rem(i, H)).start()

            @pl.when(i == mine)
            def _():
                s.arr_o[c] = s.stage_o[slot, i]

        each(n_dev, send)

    slots(back)
    spread_start(s.full_r, 1)
    spread_column(s.full_r, 1)
    spread_across(s.full_r, 1)
    slots(turn_back)
    spread_take(s.full_r, 1)
    rows_of(s.full_r, r_rows)
    for t in range(n_deep):
        cols = pl.ds(t * deep, deep)
        grad = mm_t(r_rows[...], s.dic[cols, :])
        left[pl.ds(rows, rows), cols] = jnp.where(s.pre[:, cols] > 0.0, grad, 0.0).astype(BF16)

    either(ext_mine, lambda n: wait_here(s.arr_o.at[pl.ds(0, n)], s.to_rs.at[0]), C - 1, C - 2)
    out_cols[...] = s.arr_o[...]

    for a, arr in enumerate((s.gx, s.gu)):
        cols_drain(arr, a)
    for a, full in enumerate((s.full_n, s.full_r)):
        spread_drain(full, a)
    for a in range(3):
        sum_drain(a)
    slots(lambda slot, k: wait_sent(s.stage_o.at[slot, pl.ds(0, n_dev - 1)], s.to_ss.at[slot]))


def run_group(L, H, *args):
    codes, dic = args[0], args[2]
    rows, own_width = codes.shape
    units, width = dic.shape
    C = rows // ROWS
    K = C // H
    Z = L // 2
    n_dev = L * H
    pad = -(-own_width // LANES) * LANES
    per = LANES // (own_width - LANES)
    high = rows + PACK * -(-(rows // PACK) // per)
    V, D, R = pltpu.VMEM, pltpu.SemaphoreType.DMA, ROWS
    scratch = dict(
        codes_x=V((rows, own_width), jnp.int32), codes_u=V((rows, own_width), jnp.int32),
        ebias=V((1, units), F32), dbias=V((width,), F32), gain=V((width,), F32),
        dic=V((units, width), BF16), gate=V((units, width), BF16),
        up=V((units, width), BF16), down=V((units, width), BF16),
        gx=V((n_dev, high, LANES), BF16), gu=V((n_dev, high, LANES), BF16),
        full_x=V((C, R, width), BF16), full_n=V((C, R, width), BF16), full_r=V((C, R, width), BF16),
        u_rows=V((rows, width), BF16), n_rows=V((rows, width), BF16),
        pre=V((rows, units), F32), hgrad=V((rows, units), F32), hid=V((rows, units), BF16),
        ggrad=V((rows, units), BF16), ugrad=V((rows, units), BF16),
        own=V((3, C, R, width), F32), xbuf=V((3, K, R, width), BF16),
        sib=V((3, K, R, width), F32), comb=V((3, K, R, width), BF16),
        rbuf=V((3, 2, Z, R, width), BF16), acc=V((3, 2, R, width), F32),
        rebuilt=V((2, R, width), F32), inverse=V((2, R, LANES), F32),
        stage_o=V((2, n_dev, R, pad), BF16), arr_o=V((C, R, pad), BF16),
        load_sem=D((9,)),
        col_ss=D((2,)), col_rs=D((2, L)), col_fs=D((2,)), col_fr=D((2,)),
        ag_ss=D((2, 2)), ag_xs=D((2,)), ag_xr=D((2, Z + 1)), ag_rr=D((2, Z + 1)), ag_fs=D((2,)), ag_fr=D((2,)),
        rs_cs=D((3,)), rs_cr=D((3,)), rs_ss=D((3,)), rs_rr=D((3, 2)), rs_xs=D((3,)), rs_xr=D((3, Z + 1)),
        to_ss=D((2,)), to_rs=D((1,)),
    )
    names = list(scratch)

    def body(*refs):
        group_kernel(L, H, refs[:9], refs[9:12], types.SimpleNamespace(**dict(zip(names, refs[12:]))))

    hbm = pl.BlockSpec(memory_space=pltpu.HBM)
    vm = pl.BlockSpec(memory_space=pltpu.VMEM)
    cols, left, right = pl.pallas_call(
        body,
        name="group_step",
        out_shape=(
            V((C, R, pad), BF16),
            V((2 * rows, units), BF16),
            V((2 * rows, width), BF16),
        ),
        in_specs=[hbm] * 9,
        out_specs=(vm, vm, vm),
        scratch_shapes=[scratch[n] for n in names],
        compiler_params=pltpu.CompilerParams(collective_id=0, has_side_effects=True, vmem_limit_bytes=60 * 2**20),
    )(*args)

    step = width // 6 if width % (6 * LANES) == 0 else LANES
    n_step = width // step

    def product(cols, left, right, block, grad, tiles, sem):
        copies = []
        for t in range(n_step):
            at = slice(t * step, (t + 1) * step)
            tiles[t] = lax.dot_general(
                left[...], right[:, at], (((0,), (0,)), ((), ())), preferred_element_type=F32
            ).astype(BF16)
            copies.append(pltpu.make_async_copy(tiles.at[t], grad.at[:, at], sem.at[t]))
            copies[-1].start()
        block[...] = cols[...].astype(F32).reshape(rows, pad)[:, :own_width].astype(BF16)
        for cp in copies:
            cp.wait()

    return pl.pallas_call(
        product,
        name="dictionary_product",
        out_shape=(
            jax.ShapeDtypeStruct((rows, own_width), BF16),
            jax.ShapeDtypeStruct((units, width), BF16),
        ),
        in_specs=[vm, vm, vm],
        out_specs=(vm, pl.BlockSpec(memory_space=pl.ANY)),
        scratch_shapes=[V((n_step, units, step), BF16), D((n_step,))],
        compiler_params=pltpu.CompilerParams(vmem_limit_bytes=16 * 2**20),
    )(cols, left, right)


def fits(L, H, rows, own_width, width, units, units_mlp):
    rest = own_width - LANES
    if H != 2 or rows % (ROWS * H) or rows % PACK or width % LANES or units % LANES or units != units_mlp:
        return False
    if rest <= 0 or rest >= LANES or LANES % rest or own_width * L * H != width:
        return False
    return L >= 6 and L % 2 == 0 and 0 <= rows // ROWS // H - L <= 1


CODE_STEP = 2.0 ** (-6)
NORM_EPSILON = 1e-06
GELU_ROOT = 0.7978845608028654
GELU_CUBIC = 0.044715
ACROSS = (((1,), (1,)), ((), ()))
DOWNWARD = (((0,), (0,)), ((), ()))


def gelu_parts(values):
    argument = GELU_ROOT * (values + GELU_CUBIC * values * values * values)
    tanh_value = jnp.tanh(argument)
    result = 0.5 * values * (1.0 + tanh_value)
    derivative = 0.5 * (1.0 + tanh_value) + 0.5 * values * (
        1.0 - tanh_value * tanh_value
    ) * GELU_ROOT * (1.0 + 3.0 * GELU_CUBIC * values * values)
    return (result, derivative)


def per_device(
    input_codes,
    cotangent_codes,
    dictionary,
    encoder_bias,
    decoder_bias,
    norm_gain,
    gate_weight,
    up_weight,
    down_weight,
):
    L, H = lax.axis_size("latent"), lax.axis_size("hidden")
    rows, width = input_codes.shape[0], dictionary.shape[1]
    if fits(L, H, rows, input_codes.shape[1], width, dictionary.shape[0], gate_weight.shape[0]):
        return run_group(
            L, H, input_codes, cotangent_codes, dictionary, encoder_bias[None, :], decoder_bias,
            norm_gain, gate_weight, up_weight, down_weight,
        )
    own_width = input_codes.shape[1]
    model_width = own_width * lax.axis_size(("latent", "hidden"))
    cotangent_local = (cotangent_codes.astype(jnp.float32) * CODE_STEP).astype(jnp.bfloat16)
    hidden_grad = None
    inputs_local = (input_codes.astype(jnp.float32) * CODE_STEP).astype(jnp.bfloat16)
    inputs = lax.all_gather(inputs_local, ("latent", "hidden"), axis=1, tiled=True)
    preact = (
        lax.dot_general(inputs, dictionary, ACROSS, preferred_element_type=jnp.float32)
        + encoder_bias
    )
    latents = jnp.maximum(preact, 0.0).astype(jnp.bfloat16)
    partial_value = jnp.dot(latents, dictionary, preferred_element_type=jnp.float32)
    rebuilt = lax.psum(partial_value, ("latent", "hidden")) + decoder_bias
    inverse = lax.rsqrt(
        jnp.sum(rebuilt * rebuilt, axis=1, keepdims=True) / model_width + NORM_EPSILON
    )
    normed = (rebuilt * inverse * norm_gain).astype(jnp.bfloat16)
    target = inputs.astype(jnp.float32)
    gate_proj = lax.dot_general(normed, gate_weight, ACROSS, preferred_element_type=jnp.float32)
    up_proj = lax.dot_general(normed, up_weight, ACROSS, preferred_element_type=jnp.float32)
    gelu_value, gelu_slope = gelu_parts(gate_proj)
    hidden = (gelu_value * up_proj).astype(jnp.bfloat16)
    output_terms = jnp.dot(hidden, down_weight, preferred_element_type=jnp.float32)
    block_output = lax.psum_scatter(
        output_terms, ("latent", "hidden"), scatter_dimension=1, tiled=True
    ).astype(jnp.bfloat16)
    hidden_grad = lax.dot_general(
        lax.all_gather(cotangent_local, ("latent", "hidden"), axis=1, tiled=True),
        down_weight,
        ACROSS,
        preferred_element_type=jnp.float32,
    )
    gate_grad = (hidden_grad * up_proj * gelu_slope).astype(jnp.bfloat16)
    up_grad = (hidden_grad * gelu_value).astype(jnp.bfloat16)
    partial_grad = jnp.dot(gate_grad, gate_weight, preferred_element_type=jnp.float32) + jnp.dot(
        up_grad, up_weight, preferred_element_type=jnp.float32
    )
    scaled = lax.psum(partial_grad, ("latent", "hidden")) * norm_gain
    inner_row = jnp.sum(scaled * rebuilt, axis=1, keepdims=True)
    inverse_cube = inverse * inverse * inverse
    rebuilt_grad = (
        inverse * scaled - inverse_cube * rebuilt * (inner_row / model_width) + (rebuilt - target)
    ).astype(jnp.bfloat16)
    latent_grad = lax.dot_general(
        rebuilt_grad, dictionary, ACROSS, preferred_element_type=jnp.float32
    )
    preact_grad = jnp.where(preact > 0.0, latent_grad, 0.0).astype(jnp.bfloat16)
    dictionary_grad = lax.dot_general(
        latents, rebuilt_grad, DOWNWARD, preferred_element_type=jnp.float32
    ) + lax.dot_general(preact_grad, inputs, DOWNWARD, preferred_element_type=jnp.float32)
    return (block_output, dictionary_grad.astype(jnp.bfloat16))


def solution(mesh):
    in_specs = (
        P("groups", ("latent", "hidden")),
        P("groups", ("latent", "hidden")),
        P(("latent", "hidden"), None),
        P(("latent", "hidden")),
        P(),
        P(),
        P(("latent", "hidden"), None),
        P(("latent", "hidden"), None),
        P(("latent", "hidden"), None),
    )
    out_specs = (P("groups", ("latent", "hidden")), P(("latent", "hidden"), "groups"))
    return jax.shard_map(
        per_device, mesh=mesh, in_specs=in_specs, out_specs=out_specs, check_vma=False
    )
```

time: 80.1 us -> 72.1 us (0.900)
  Pallas kernels: 79.3 us -> 71.3 us
    pallas_call x2, Pallas kernels: 79.3 us -> 71.3 us  [the longest x1 68.2 us: run_group(): pl.pallas_call(body, name='group_step', out_shape=(V((C, R, pad), BF16),...]
where the time goes in v1:
time: 72.1 us; the launch traced here: 71.9 us
  Pallas kernels  71.3 us (99%)
    pallas_call x1, Pallas kernels, run_group(): pl.pallas_call(body, name='group_step', out_shape=(V((C, R, pad), BF16),...  68.2 us
    pallas_call x1, Pallas kernels, run_group(): pl.pallas_call(product, name='dictionary_product', out_shape=(jax.ShapeDt...  3.06 us

profile of v1, /device:TPU:0, one launch (start us, length us, event | category | flops | bytes accessed | tf_op | source)
XLA Modules:
  0.0 71.9 jit_solution(11235894212822218843)
XLA Ops:
  0.6 68.2 %group_step.1 = (bf16[18,8,256]{2,1,0:T(8,128)(2,1)S(1)}, bf16[288,512]{1,0:T(8,128)(2,1)S(1)}, bf16[288,2304]{1,0:T(8,128)(2,1)S(1)}) custom-call(s32[144,144]{1,0:T(8,128)} %refs_0_.1, s32[144,144]{1,0:T(8,128)} %refs_1_.1, bf16[512,2304]{1,0:T(8,128)(2,1)} %refs_2_.1, f32[1,512]{1,0:T(1,128)} %bitcast.1, f32[2304]{0:T(1024)} %refs_4_.1, f32[2304]{0:T(1024)} %refs_5_.1, ...), custom_call_target="tpu_custom_call" | custom-call | tf_op jit(solution)/shard_map/group_step/pallas_call | solution.py:487
  68.9 3.1 %dictionary_product.1 = (bf16[144,144]{1,0:T(8,128)(2,1)}, bf16[512,2304]{1,0:T(8,128)(2,1)}) custom-call(bf16[18,8,256]{2,1,0:T(8,128)(2,1)S(1)} %get-tuple-element.5.cols, bf16[288,512]{1,0:T(8,128)(2,1)S(1)} %get-tuple-element.6.left, bf16[288,2304]{1,0:T(8,128)(2,1)S(1)} %get-tuple-element.7.right), custom_call_target="tpu_custom_call" | custom-call | tf_op jit(solution)/shard_map/dictionary_product/pallas_call | solution.py:517

commit v2 on v1

--- a/solution.py
+++ b/solution.py
@@ -30,7 +30,7 @@
     extra = K - L
     n_dev = L * H
     mine = me * H + h
-    pad = out_cols.shape[2]
+    high = s.gx.shape[1]
     rest = own_width - LANES
     per = LANES // rest
 
@@ -94,20 +94,17 @@
     Z = L // X
     z, x = me // X, lax.rem(me, X)
     across_me = z * X + 1 - x
-
-    def peer(j):
-        if Z == 4:
-            return (z + 1 - 2 * lax.rem(z, 2), z + 2 - 4 * (z // 2), 3 - z)[j]
-        return lax.rem(z + 1 + j, Z)
-
-    def in_column(j):
-        return peer(j) * X + x
-
-    def beside(j):
-        return peer(j) * X + 1 - x
-
-    near = range(Z - 1)
-    far = (1, 2, 0) if Z == 4 else near
+    near_z, same_z, flip_z = z + 1 - 2 * lax.rem(z, 2), z + 2 - 4 * (z // 2), 3 - z
+    peers = (near_z, same_z, flip_z)
+    far = (same_z, flip_z, near_z)
+
+    def col(zz):
+        return zz * X + x
+
+    def beside(zz):
+        return zz * X + 1 - x
+
+    ext_z = ext(h) // X
     ext_here = lax.rem(ext(h), X) == x
     ext_mine = me == ext(h)
     ext_passes = jnp.logical_and(ext_here, jnp.logical_not(ext_mine))
@@ -124,21 +121,46 @@
     def wait_sent(buf, sem):
         rcopy(buf, buf, sem, sem, me, other).wait_send()
 
+    def cols_send(arr, a, i, lat):
+        rcopy(arr.at[i], arr.at[i], s.col_ss.at[a], s.col_rs.at[a, i // H], lat, h).start()
+
+    def cols_give(arr, a, i):
+        rcopy(arr.at[i], arr.at[i], s.col_fs.at[a], s.col_fr.at[a], me, other).start()
+
+    def cols_got(arr, a, lat, relay=False):
+        i = lat * H + h
+        wait_here(arr.at[i], s.col_rs.at[a, lat])
+        if relay:
+            cols_send(arr, a, i, across_me)
+        cols_give(arr, a, i)
+
     def cols_start(arr, a):
-        for j in far:
-            for lat in (beside(j), in_column(j)):
-                rcopy(arr.at[mine], arr.at[mine], s.col_ss.at[a], s.col_rs.at[a, me], lat, h).start()
-        rcopy(arr.at[mine], arr.at[mine], s.col_ss.at[a], s.col_rs.at[a, me], across_me, h).start()
-        rcopy(arr.at[mine], arr.at[mine], s.col_fs.at[a], s.col_fr.at[a], me, other).start()
+        for zz in far:
+            for lat in (beside(zz), col(zz)):
+                cols_send(arr, a, mine, lat)
+        cols_send(arr, a, mine, across_me)
+        cols_give(arr, a, mine)
 
     def cols_relay(arr, a):
-        order = [across_me]
-        for j in near:
-            order += [in_column(j), beside(j)]
-        for lat in order:
-            piece = arr.at[lat * H + h]
-            wait_here(piece, s.col_rs.at[a, lat])
-            rcopy(piece, piece, s.col_fs.at[a], s.col_fr.at[a], me, other).start()
+        cols_got(arr, a, across_me)
+        for zz in peers:
+            cols_got(arr, a, col(zz))
+            cols_got(arr, a, beside(zz))
+
+    def cols_lean_start(arr, a):
+        for zz in far:
+            cols_send(arr, a, mine, col(zz))
+        cols_send(arr, a, mine, across_me)
+        cols_give(arr, a, mine)
+
+    def cols_lean_column(arr, a):
+        for zz in peers:
+            cols_got(arr, a, col(zz), True)
+
+    def cols_lean_across(arr, a):
+        cols_got(arr, a, across_me)
+        for zz in peers:
+            cols_got(arr, a, beside(zz))
 
     def cols_take(arr, a):
         wait_here(arr.at[pl.ds(0, L)], s.col_fr.at[a])
@@ -188,8 +210,8 @@
         def one(slot, k):
             c = h * K + k
             i = Z if slot else z
-            for j in far:
-                rcopy(full.at[c], full.at[c], s.ag_ss.at[a, slot], s.ag_rr.at[a, i], in_column(j), h).start()
+            for zz in far:
+                rcopy(full.at[c], full.at[c], s.ag_ss.at[a, slot], s.ag_rr.at[a, i], col(zz), h).start()
             step_across(full, a, k, i)
             hand_over(full, a, k)
 
@@ -205,30 +227,27 @@
         hand_over(full, a, k)
 
     def spread_column(full, a):
-        for j in near:
-            relay_column(full, a, in_column(j), peer(j))
+        for zz in peers:
+            relay_column(full, a, col(zz), zz)
         when_extra(ext_passes, lambda k, i: relay_column(full, a, k, i))
 
     def spread_across(full, a):
         relay_across(full, a, across_me, z)
-        for j in near:
-            relay_across(full, a, beside(j), peer(j))
+        for zz in peers:
+            relay_across(full, a, beside(zz), zz)
         when_extra(jnp.logical_not(ext_here), lambda k, i: relay_across(full, a, k, i))
 
     def spread_take(full, a):
         wait_here(full.at[pl.ds(other * K, K)], s.ag_fr.at[a])
 
-    def either(cond, body, less, more):
-        if extra:
-            @pl.when(cond)
-            def _():
-                body(more)
-
-            @pl.when(jnp.logical_not(cond))
-            def _():
-                body(less)
-        else:
-            body(less)
+    def either(cond, body, no, yes):
+        @pl.when(cond)
+        def _():
+            body(yes)
+
+        @pl.when(jnp.logical_not(cond))
+        def _():
+            body(no)
 
     def spread_drain(full, a):
         slots(lambda slot, k: wait_sent(full.at[pl.ds(0, Z - 1)], s.ag_ss.at[a, slot]))
@@ -260,8 +279,8 @@
             s.comb[a, k] = sum_chip(a, k).astype(BF16)
             rcopy(s.comb.at[a, k], s.xbuf.at[a, k], s.rs_xs.at[a], s.rs_xr.at[a, i], across_me, h).start()
 
-        for j in far:
-            leave(beside(j), peer(j))
+        for zz in far:
+            leave(beside(zz), zz)
         when_extra(jnp.logical_not(ext_here), leave)
         leave(across_me, z)
 
@@ -275,8 +294,8 @@
             s.comb[a, k] = total(k, i).astype(BF16)
             rcopy(s.comb.at[a, k], s.rbuf.at[a, slot, z], s.rs_ss.at[a], s.rs_rr.at[a, slot], owner, h).start()
 
-        for j in far:
-            leave(0, in_column(j), peer(j), in_column(j))
+        for zz in far:
+            leave(0, col(zz), zz, col(zz))
         when_extra(ext_passes, lambda k, i: leave(1, k, i, ext(h)))
         s.acc[a, 0] = total(me, z)
 
@@ -288,14 +307,75 @@
     def sum_value(a, slot):
         value = s.acc[a, slot]
         wait_here(s.rbuf.at[a, slot, pl.ds(0, Z - 1)], s.rs_rr.at[a, slot])
-        for j in near:
-            value = value + s.rbuf[a, slot, peer(j)].astype(F32)
+        for zz in peers:
+            value = value + s.rbuf[a, slot, zz].astype(F32)
         return value
 
     def sum_drain(a):
         wait_sent(s.sib.at[a], s.rs_cs.at[a])
         either(jnp.logical_not(ext_here), lambda n: wait_sent(s.xbuf.at[a, pl.ds(0, n)], s.rs_xs.at[a]), Z, Z + 1)
         either(ext_passes, lambda n: wait_sent(s.xbuf.at[a, pl.ds(0, n)], s.rs_ss.at[a]), Z - 1, Z)
+
+    def out_tile(t, value):
+        s.wide_out[:, t * wide : (t + 1) * wide] = value
+
+    def out_pieces():
+        lane = lax.broadcasted_iota(jnp.int32, (rows, LANES), 1)
+        group = lax.broadcasted_iota(jnp.int32, (PACK, LANES), 1) // rest
+        for i in range(n_dev):
+            first, offset = divmod(i * own_width, LANES)
+            here = s.wide_out[:, first * LANES : (first + 1) * LANES]
+            there = s.wide_out[:, (first + 1) * LANES : (first + 2) * LANES]
+            piece = s.own_out.at[i % H, i // H]
+            piece[pl.ds(0, rows)] = jnp.where(lane >= offset, here, there) if offset else here
+            for b in range(high // PACK - rows // PACK):
+                packed = jnp.zeros((PACK, LANES), F32)
+                for g in range(b * per, min((b + 1) * per, rows // PACK)):
+                    part = there[g * PACK : (g + 1) * PACK]
+                    move = ((g % per) * rest - offset) % LANES
+                    part = pltpu.roll(part, move, 1) if move else part
+                    packed = jnp.where(group == g % per, part, packed)
+                piece[pl.ds(rows + b * PACK, PACK)] = packed
+        rcopy(s.own_out.at[other], s.sib_out, s.out_cs.at[0], s.out_cr.at[0], me, other).start()
+
+    def out_chip(lat):
+        return s.own_out[h, lat] + s.sib_out[lat]
+
+    def out_middle():
+        wait_here(s.sib_out, s.out_cr.at[0])
+        for lat, i in [(beside(zz), zz) for zz in far] + [(across_me, z)]:
+            s.comb_out[lat] = out_chip(lat).astype(BF16)
+            rcopy(s.comb_out.at[lat], s.xbuf_out.at[lat], s.out_xs.at[0], s.out_xr.at[i], across_me, h).start()
+
+    def out_total(lat, i):
+        wait_here(s.xbuf_out.at[lat], s.out_xr.at[i])
+        return out_chip(lat) + s.xbuf_out[lat].astype(F32)
+
+    def out_cross():
+        for zz in far:
+            lat = col(zz)
+            s.comb_out[lat] = out_total(lat, zz).astype(BF16)
+            rcopy(s.comb_out.at[lat], s.rbuf_out.at[z], s.out_ss.at[0], s.out_rr.at[0], lat, h).start()
+        s.acc_out[...] = out_total(me, z)
+
+    def out_final():
+        wait_here(s.rbuf_out.at[pl.ds(0, Z - 1)], s.out_rr.at[0])
+        value = s.acc_out[...]
+        for zz in peers:
+            value = value + s.rbuf_out[zz].astype(F32)
+        back_by = lax.rem(LANES - lax.rem(mine * own_width, LANES), LANES)
+        out_cols[:, :LANES] = pltpu.roll(value[:rows], back_by, 1).astype(BF16)
+        parts = []
+        for g in range(rows // PACK):
+            part = value[rows + (g // per) * PACK : rows + (g // per + 1) * PACK]
+            move = (-(g % per) * rest) % LANES
+            parts.append(pltpu.roll(part, move, 1) if move else part)
+        out_cols[:, LANES:] = jnp.concatenate(parts, axis=0)[:, :rest].astype(BF16)
+
+    def out_drain():
+        wait_sent(s.sib_out, s.out_cs.at[0])
+        wait_sent(s.xbuf_out.at[pl.ds(0, Z)], s.out_xs.at[0])
+        wait_sent(s.xbuf_out.at[pl.ds(0, Z - 1)], s.out_ss.at[0])
 
     across = (((1,), (1,)), ((), ()))
 
@@ -315,7 +395,7 @@
     loads[1].wait()
     stage(s.codes_u, s.gu)
     cols_relay(s.gx, 0)
-    cols_start(s.gu, 1)
+    cols_lean_start(s.gu, 1)
     cols_take(s.gx, 0)
     x_rows = right.at[pl.ds(rows, rows)]
     r_rows = right.at[pl.ds(0, rows)]
@@ -334,20 +414,14 @@
         left[pl.ds(0, rows), cols] = jnp.maximum(pre, 0.0).astype(BF16)
     for t in range(n_wide):
         sum_tile(0, t, mm(left[pl.ds(0, rows), :], s.dic[:, t * wide : (t + 1) * wide]))
-    cols_relay(s.gu, 1)
     sum_start(0)
     sum_middle(0)
     sum_cross(0)
-    cols_take(s.gu, 1)
+    cols_lean_column(s.gu, 1)
 
     def put_u(t, value):
         s.u_rows[:, t * LANES : (t + 1) * LANES] = value.astype(BF16)
 
-    cols_rows(s.gu, put_u)
-    loads[6].wait()
-    for t in range(n_deep):
-        cols = pl.ds(t * deep, deep)
-        s.hgrad[:, cols] = mm_t(s.u_rows[...], s.down[cols, :])
     loads[4].wait()
     loads[5].wait()
 
@@ -360,6 +434,13 @@
 
     slots(norm)
     spread_start(s.full_n, 0)
+    cols_lean_across(s.gu, 1)
+    cols_take(s.gu, 1)
+    cols_rows(s.gu, put_u)
+    loads[6].wait()
+    for t in range(n_deep):
+        cols = pl.ds(t * deep, deep)
+        s.hgrad[:, cols] = mm_t(s.u_rows[...], s.down[cols, :])
     loads[7].wait()
     loads[8].wait()
     spread_column(s.full_n, 0)
@@ -385,11 +466,10 @@
     sum_start(1)
     sum_middle(1)
     for t in range(n_wide):
-        sum_tile(2, t, mm(s.hid[...], s.down[:, t * wide : (t + 1) * wide]))
-    sum_start(2)
+        out_tile(t, mm(s.hid[...], s.down[:, t * wide : (t + 1) * wide]))
+    out_pieces()
     sum_cross(1)
-    sum_middle(2)
-    sum_cross(2)
+    out_middle()
 
     def back(slot, k):
         scaled = sum_value(1, slot) * s.gain[...]
@@ -401,30 +481,11 @@
             inverse * scaled - inverse * inverse * inverse * rebuilt * (inner / width) + (rebuilt - target)
         ).astype(BF16)
 
-    def turn_back(slot, k):
-        value = sum_value(2, slot)
-        c = h * K + k
-        for i in range(n_dev):
-            piece = value[:, i * own_width : (i + 1) * own_width]
-            piece = jnp.concatenate([piece, jnp.zeros((ROWS, pad - own_width), F32)], axis=1)
-            s.stage_o[slot, i] = piece.astype(BF16)
-
-        def send(i):
-            @pl.when(i != mine)
-            def _():
-                rcopy(s.stage_o.at[slot, i], s.arr_o.at[c], s.to_ss.at[slot], s.to_rs.at[0], i // H, lax.rem(i, H)).start()
-
-            @pl.when(i == mine)
-            def _():
-                s.arr_o[c] = s.stage_o[slot, i]
-
-        each(n_dev, send)
-
     slots(back)
     spread_start(s.full_r, 1)
     spread_column(s.full_r, 1)
+    out_cross()
     spread_across(s.full_r, 1)
-    slots(turn_back)
     spread_take(s.full_r, 1)
     rows_of(s.full_r, r_rows)
     for t in range(n_deep):
@@ -432,16 +493,14 @@
         grad = mm_t(r_rows[...], s.dic[cols, :])
         left[pl.ds(rows, rows), cols] = jnp.where(s.pre[:, cols] > 0.0, grad, 0.0).astype(BF16)
 
-    either(ext_mine, lambda n: wait_here(s.arr_o.at[pl.ds(0, n)], s.to_rs.at[0]), C - 1, C - 2)
-    out_cols[...] = s.arr_o[...]
-
+    out_final()
     for a, arr in enumerate((s.gx, s.gu)):
         cols_drain(arr, a)
     for a, full in enumerate((s.full_n, s.full_r)):
         spread_drain(full, a)
-    for a in range(3):
+    for a in range(2):
         sum_drain(a)
-    slots(lambda slot, k: wait_sent(s.stage_o.at[slot, pl.ds(0, n_dev - 1)], s.to_ss.at[slot]))
+    out_drain()
 
 
 def run_group(L, H, *args):
@@ -452,7 +511,6 @@
     K = C // H
     Z = L // 2
     n_dev = L * H
-    pad = -(-own_width // LANES) * LANES
     per = LANES // (own_width - LANES)
     high = rows + PACK * -(-(rows // PACK) // per)
     V, D, R = pltpu.VMEM, pltpu.SemaphoreType.DMA, ROWS
@@ -466,16 +524,18 @@
         u_rows=V((rows, width), BF16), n_rows=V((rows, width), BF16),
         pre=V((rows, units), F32), hgrad=V((rows, units), F32), hid=V((rows, units), BF16),
         ggrad=V((rows, units), BF16), ugrad=V((rows, units), BF16),
-        own=V((3, C, R, width), F32), xbuf=V((3, K, R, width), BF16),
-        sib=V((3, K, R, width), F32), comb=V((3, K, R, width), BF16),
-        rbuf=V((3, 2, Z, R, width), BF16), acc=V((3, 2, R, width), F32),
+        own=V((2, C, R, width), F32), xbuf=V((2, K, R, width), BF16),
+        sib=V((2, K, R, width), F32), comb=V((2, K, R, width), BF16),
+        rbuf=V((2, 2, Z, R, width), BF16), acc=V((2, 2, R, width), F32),
         rebuilt=V((2, R, width), F32), inverse=V((2, R, LANES), F32),
-        stage_o=V((2, n_dev, R, pad), BF16), arr_o=V((C, R, pad), BF16),
+        wide_out=V((rows, width), F32), own_out=V((H, L, high, LANES), F32), sib_out=V((L, high, LANES), F32),
+        comb_out=V((L, high, LANES), BF16), xbuf_out=V((L, high, LANES), BF16),
+        rbuf_out=V((Z, high, LANES), BF16), acc_out=V((high, LANES), F32),
         load_sem=D((9,)),
         col_ss=D((2,)), col_rs=D((2, L)), col_fs=D((2,)), col_fr=D((2,)),
         ag_ss=D((2, 2)), ag_xs=D((2,)), ag_xr=D((2, Z + 1)), ag_rr=D((2, Z + 1)), ag_fs=D((2,)), ag_fr=D((2,)),
-        rs_cs=D((3,)), rs_cr=D((3,)), rs_ss=D((3,)), rs_rr=D((3, 2)), rs_xs=D((3,)), rs_xr=D((3, Z + 1)),
-        to_ss=D((2,)), to_rs=D((1,)),
+        rs_cs=D((2,)), rs_cr=D((2,)), rs_ss=D((2,)), rs_rr=D((2, 2)), rs_xs=D((2,)), rs_xr=D((2, Z + 1)),
+        out_cs=D((1,)), out_cr=D((1,)), out_xs=D((1,)), out_xr=D((Z,)), out_ss=D((1,)), out_rr=D((1,)),
     )
     names = list(scratch)
 
@@ -488,7 +548,7 @@
         body,
         name="group_step",
         out_shape=(
-            V((C, R, pad), BF16),
+            V((rows, own_width), BF16),
             V((2 * rows, units), BF16),
             V((2 * rows, width), BF16),
         ),
@@ -510,7 +570,7 @@
             ).astype(BF16)
             copies.append(pltpu.make_async_copy(tiles.at[t], grad.at[:, at], sem.at[t]))
             copies[-1].start()
-        block[...] = cols[...].astype(F32).reshape(rows, pad)[:, :own_width].astype(BF16)
+        block[...] = cols[...]
         for cp in copies:
             cp.wait()
 
@@ -534,7 +594,7 @@
         return False
     if rest <= 0 or rest >= LANES or LANES % rest or own_width * L * H != width:
         return False
-    return L >= 6 and L % 2 == 0 and 0 <= rows // ROWS // H - L <= 1
+    return L == 8 and rows // ROWS // H == L + 1
 
 
 CODE_STEP = 2.0 ** (-6)

time: 72.1 us -> 66.6 us (0.924)
  Pallas kernels: 71.3 us -> 65.9 us
    pallas_call x1, Pallas kernels: 68.2 us -> 62.8 us  [run_group(): pl.pallas_call(body, name='group_step', out_shape=(V((rows, own_width), B...]
where the time goes in v2:
time: 66.6 us; the launch traced here: 66.5 us
  Pallas kernels  65.9 us (99%)
    pallas_call x1, Pallas kernels, run_group(): pl.pallas_call(body, name='group_step', out_shape=(V((rows, own_width), B...  62.8 us
    pallas_call x1, Pallas kernels, run_group(): pl.pallas_call(product, name='dictionary_product', out_shape=(jax.ShapeDt...  3.06 us

profile of v2, /device:TPU:0, one launch (start us, length us, event | category | flops | bytes accessed | tf_op | source)
XLA Modules:
  0.0 66.5 jit_solution(16648214741748258874)
XLA Ops:
  0.6 62.8 %group_step.1 = (bf16[144,144]{1,0:T(8,128)(2,1)S(1)}, bf16[288,512]{1,0:T(8,128)(2,1)S(1)}, bf16[288,2304]{1,0:T(8,128)(2,1)S(1)}) custom-call(s32[144,144]{1,0:T(8,128)} %refs_0_.1, s32[144,144]{1,0:T(8,128)} %refs_1_.1, bf16[512,2304]{1,0:T(8,128)(2,1)} %refs_2_.1, f32[1,512]{1,0:T(1,128)} %bitcast.1, f32[2304]{0:T(1024)} %refs_4_.1, f32[2304]{0:T(1024)} %refs_5_.1, ...), custom_call_target="tpu_custom_call" | custom-call | tf_op jit(solution)/shard_map/group_step/pallas_call | solution.py:547
  63.4 3.1 %dictionary_product.1 = (bf16[144,144]{1,0:T(8,128)(2,1)}, bf16[512,2304]{1,0:T(8,128)(2,1)}) custom-call(bf16[144,144]{1,0:T(8,128)(2,1)S(1)} %get-tuple-element.5.cols, bf16[288,512]{1,0:T(8,128)(2,1)S(1)} %get-tuple-element.6.left, bf16[288,2304]{1,0:T(8,128)(2,1)S(1)} %get-tuple-element.7.right), custom_call_target="tpu_custom_call" | custom-call | tf_op jit(solution)/shard_map/dictionary_product/pallas_call | solution.py:577

commit v3 on v2

--- a/solution.py
+++ b/solution.py
@@ -467,8 +467,8 @@
     sum_middle(1)
     for t in range(n_wide):
         out_tile(t, mm(s.hid[...], s.down[:, t * wide : (t + 1) * wide]))
+    sum_cross(1)
     out_pieces()
-    sum_cross(1)
     out_middle()
 
     def back(slot, k):

time: 66.6 us -> 64.3 us (0.965)
  Pallas kernels: 65.9 us -> 63.5 us
    pallas_call x1, Pallas kernels: 62.8 us -> 60.4 us  [run_group(): pl.pallas_call(body, name='group_step', out_shape=(V((rows, own_width), B...]
where the time goes in v3:
time: 64.3 us; the launch traced here: 64.1 us
  Pallas kernels  63.5 us (99%)
    pallas_call x1, Pallas kernels, run_group(): pl.pallas_call(body, name='group_step', out_shape=(V((rows, own_width), B...  60.4 us
    pallas_call x1, Pallas kernels, run_group(): pl.pallas_call(product, name='dictionary_product', out_shape=(jax.ShapeDt...  3.06 us

profile of v3, /device:TPU:0, one launch (start us, length us, event | category | flops | bytes accessed | tf_op | source)
XLA Modules:
  0.0 64.1 jit_solution(1171242744291378443)
XLA Ops:
  0.6 60.4 %group_step.1 = (bf16[144,144]{1,0:T(8,128)(2,1)S(1)}, bf16[288,512]{1,0:T(8,128)(2,1)S(1)}, bf16[288,2304]{1,0:T(8,128)(2,1)S(1)}) custom-call(s32[144,144]{1,0:T(8,128)} %refs_0_.1, s32[144,144]{1,0:T(8,128)} %refs_1_.1, bf16[512,2304]{1,0:T(8,128)(2,1)} %refs_2_.1, f32[1,512]{1,0:T(1,128)} %bitcast.1, f32[2304]{0:T(1024)} %refs_4_.1, f32[2304]{0:T(1024)} %refs_5_.1, ...), custom_call_target="tpu_custom_call" | custom-call | tf_op jit(solution)/shard_map/group_step/pallas_call | solution.py:547
  61.0 3.1 %dictionary_product.1 = (bf16[144,144]{1,0:T(8,128)(2,1)}, bf16[512,2304]{1,0:T(8,128)(2,1)}) custom-call(bf16[144,144]{1,0:T(8,128)(2,1)S(1)} %get-tuple-element.5.cols, bf16[288,512]{1,0:T(8,128)(2,1)S(1)} %get-tuple-element.6.left, bf16[288,2304]{1,0:T(8,128)(2,1)S(1)} %get-tuple-element.7.right), custom_call_target="tpu_custom_call" | custom-call | tf_op jit(solution)/shard_map/dictionary_product/pallas_call | solution.py:577

commit v4 on v3

--- a/solution.py
+++ b/solution.py
@@ -9,6 +9,7 @@
 
 ROWS = 8
 PACK = 16
+PARTS = 1
 LANES = 128
 TILE = 256
 MESH = pl.DeviceIdType.MESH
@@ -136,28 +137,15 @@
 
     def cols_start(arr, a):
         for zz in far:
-            for lat in (beside(zz), col(zz)):
-                cols_send(arr, a, mine, lat)
-        cols_send(arr, a, mine, across_me)
-        cols_give(arr, a, mine)
-
-    def cols_relay(arr, a):
-        cols_got(arr, a, across_me)
-        for zz in peers:
-            cols_got(arr, a, col(zz))
-            cols_got(arr, a, beside(zz))
-
-    def cols_lean_start(arr, a):
-        for zz in far:
             cols_send(arr, a, mine, col(zz))
         cols_send(arr, a, mine, across_me)
         cols_give(arr, a, mine)
 
-    def cols_lean_column(arr, a):
+    def cols_column(arr, a):
         for zz in peers:
             cols_got(arr, a, col(zz), True)
 
-    def cols_lean_across(arr, a):
+    def cols_across(arr, a):
         cols_got(arr, a, across_me)
         for zz in peers:
             cols_got(arr, a, beside(zz))
@@ -198,47 +186,57 @@
                         value = jnp.where(lane >= offset, value, main(i))
             put(t, value)
 
-    def hand_over(full, a, k):
-        c = h * K + k
-        rcopy(full.at[c], full.at[c], s.ag_fs.at[a], s.ag_fr.at[a], me, other).start()
-
-    def step_across(full, a, k, i):
-        c = h * K + k
-        rcopy(full.at[c], full.at[c], s.ag_xs.at[a], s.ag_xr.at[a, i], across_me, h).start()
-
-    def spread_start(full, a):
+    part_width = width // PARTS
+
+    def part(full, c, p):
+        return full.at[c, :, pl.ds(p * part_width, part_width)]
+
+    def hand_over(full, a, k, p):
+        piece = part(full, h * K + k, p)
+        rcopy(piece, piece, s.ag_fs.at[a], s.ag_fr.at[a, p], me, other).start()
+
+    def step_across(full, a, k, i, p):
+        piece = part(full, h * K + k, p)
+        rcopy(piece, piece, s.ag_xs.at[a], s.ag_xr.at[a, i, p], across_me, h).start()
+
+    def spread_start(full, a, ready=None):
         def one(slot, k):
+            if ready is not None:
+                ready(slot, k)
             c = h * K + k
             i = Z if slot else z
-            for zz in far:
-                rcopy(full.at[c], full.at[c], s.ag_ss.at[a, slot], s.ag_rr.at[a, i], col(zz), h).start()
-            step_across(full, a, k, i)
-            hand_over(full, a, k)
+            for p in range(PARTS):
+                piece = part(full, c, p)
+                for zz in far:
+                    rcopy(piece, piece, s.ag_ss.at[a, slot], s.ag_rr.at[a, i, p], col(zz), h).start()
+                step_across(full, a, k, i, p)
+                hand_over(full, a, k, p)
 
         slots(one)
 
-    def relay_column(full, a, k, i):
-        wait_here(full.at[h * K + k], s.ag_rr.at[a, i])
-        step_across(full, a, k, i)
-        hand_over(full, a, k)
-
-    def relay_across(full, a, k, i):
-        wait_here(full.at[h * K + k], s.ag_xr.at[a, i])
-        hand_over(full, a, k)
+    def relay_column(full, a, k, i, p):
+        wait_here(part(full, h * K + k, p), s.ag_rr.at[a, i, p])
+        step_across(full, a, k, i, p)
+        hand_over(full, a, k, p)
+
+    def relay_across(full, a, k, i, p):
+        wait_here(part(full, h * K + k, p), s.ag_xr.at[a, i, p])
+        hand_over(full, a, k, p)
 
     def spread_column(full, a):
+        for p in range(PARTS):
+            for zz in peers:
+                relay_column(full, a, col(zz), zz, p)
+            when_extra(ext_passes, lambda k, i: relay_column(full, a, k, i, p))
+
+    def spread_across(full, a, p):
+        relay_across(full, a, across_me, z, p)
         for zz in peers:
-            relay_column(full, a, col(zz), zz)
-        when_extra(ext_passes, lambda k, i: relay_column(full, a, k, i))
-
-    def spread_across(full, a):
-        relay_across(full, a, across_me, z)
-        for zz in peers:
-            relay_across(full, a, beside(zz), zz)
-        when_extra(jnp.logical_not(ext_here), lambda k, i: relay_across(full, a, k, i))
-
-    def spread_take(full, a):
-        wait_here(full.at[pl.ds(other * K, K)], s.ag_fr.at[a])
+            relay_across(full, a, beside(zz), zz, p)
+        when_extra(jnp.logical_not(ext_here), lambda k, i: relay_across(full, a, k, i, p))
+
+    def spread_take(full, a, p):
+        wait_here(full.at[pl.ds(other * K, K), :, pl.ds(p * part_width, part_width)], s.ag_fr.at[a, p])
 
     def either(cond, body, no, yes):
         @pl.when(cond)
@@ -254,8 +252,9 @@
         either(ext_here, lambda n: wait_sent(full.at[pl.ds(0, n)], s.ag_xs.at[a]), Z, Z + 1)
         wait_sent(full.at[pl.ds(0, K)], s.ag_fs.at[a])
 
-    def rows_of(full, dst):
-        dst[...] = full[...].astype(F32).reshape(rows, width).astype(BF16)
+    def rows_of(full, dst, p):
+        at_cols = slice(p * part_width, (p + 1) * part_width)
+        dst[:, at_cols] = full[:, :, at_cols].astype(F32).reshape(rows, part_width).astype(BF16)
 
     def sum_tile(a, t, value):
         cols = pl.ds(t * wide, wide)
@@ -388,14 +387,22 @@
     deep = TILE if units % TILE == 0 else units
     n_deep = units // deep
 
+    def flip(src, dst):
+        for t in range(units // LANES):
+            at_rows = slice(t * LANES, (t + 1) * LANES)
+            dst[:, at_rows] = src[at_rows, :].T
+
     loads[0].wait()
     stage(s.codes_x, s.gx)
     pl.semaphore_wait(barrier, n_dev - 1)
     cols_start(s.gx, 0)
     loads[1].wait()
     stage(s.codes_u, s.gu)
-    cols_relay(s.gx, 0)
-    cols_lean_start(s.gu, 1)
+    loads[2].wait()
+    flip(s.dic, s.dic_t)
+    cols_column(s.gx, 0)
+    cols_across(s.gx, 0)
+    cols_start(s.gu, 1)
     cols_take(s.gx, 0)
     x_rows = right.at[pl.ds(rows, rows)]
     r_rows = right.at[pl.ds(0, rows)]
@@ -405,19 +412,22 @@
         s.full_x[:, :, t * LANES : (t + 1) * LANES] = value.reshape(C, ROWS, LANES).astype(BF16)
 
     cols_rows(s.gx, put_x)
-    loads[2].wait()
     loads[3].wait()
     for t in range(n_deep):
         cols = pl.ds(t * deep, deep)
-        pre = mm_t(x_rows[...], s.dic[cols, :]) + s.ebias[:, cols]
+        pre = mm(x_rows[...], s.dic_t[:, cols]) + s.ebias[:, cols]
         s.pre[:, cols] = pre
         left[pl.ds(0, rows), cols] = jnp.maximum(pre, 0.0).astype(BF16)
     for t in range(n_wide):
         sum_tile(0, t, mm(left[pl.ds(0, rows), :], s.dic[:, t * wide : (t + 1) * wide]))
     sum_start(0)
     sum_middle(0)
+    loads[7].wait()
+    flip(s.gate, s.gate_t)
+    loads[8].wait()
+    flip(s.up, s.up_t)
     sum_cross(0)
-    cols_lean_column(s.gu, 1)
+    cols_column(s.gu, 1)
 
     def put_u(t, value):
         s.u_rows[:, t * LANES : (t + 1) * LANES] = value.astype(BF16)
@@ -432,25 +442,35 @@
         s.inverse[slot] = jnp.broadcast_to(inverse, (ROWS, LANES))
         s.full_n[h * K + k] = (rebuilt * inverse * s.gain[...]).astype(BF16)
 
-    slots(norm)
-    spread_start(s.full_n, 0)
-    cols_lean_across(s.gu, 1)
+    spread_start(s.full_n, 0, norm)
+    cols_across(s.gu, 1)
     cols_take(s.gu, 1)
     cols_rows(s.gu, put_u)
     loads[6].wait()
     for t in range(n_deep):
         cols = pl.ds(t * deep, deep)
         s.hgrad[:, cols] = mm_t(s.u_rows[...], s.down[cols, :])
-    loads[7].wait()
-    loads[8].wait()
     spread_column(s.full_n, 0)
-    spread_across(s.full_n, 0)
-    spread_take(s.full_n, 0)
-    rows_of(s.full_n, s.n_rows)
+    for p in range(PARTS):
+        spread_across(s.full_n, 0, p)
+        spread_take(s.full_n, 0, p)
+        rows_of(s.full_n, s.n_rows, p)
+        if p < PARTS - 1:
+            at_cols = slice(p * part_width, (p + 1) * part_width)
+            for t in range(n_deep):
+                cols = pl.ds(t * deep, deep)
+                g = mm(s.n_rows[:, at_cols], s.gate_t[at_cols, cols])
+                u = mm(s.n_rows[:, at_cols], s.up_t[at_cols, cols])
+                s.g_sum[:, cols] = g + s.g_sum[:, cols] if p else g
+                s.u_sum[:, cols] = u + s.u_sum[:, cols] if p else u
+    last = slice((PARTS - 1) * part_width, width)
     for t in range(n_deep):
         cols = pl.ds(t * deep, deep)
-        g = mm_t(s.n_rows[...], s.gate[cols, :])
-        u = mm_t(s.n_rows[...], s.up[cols, :])
+        g = mm(s.n_rows[:, last], s.gate_t[last, cols])
+        u = mm(s.n_rows[:, last], s.up_t[last, cols])
+        if PARTS > 1:
+            g = g + s.g_sum[:, cols]
+            u = u + s.u_sum[:, cols]
         th = jnp.tanh(0.7978845608028654 * (g + 0.044715 * g * g * g))
         value = 0.5 * g * (1.0 + th)
         slope = 0.5 * (1.0 + th) + 0.5 * g * (1.0 - th * th) * 0.7978845608028654 * (
@@ -481,25 +501,33 @@
             inverse * scaled - inverse * inverse * inverse * rebuilt * (inner / width) + (rebuilt - target)
         ).astype(BF16)
 
-    slots(back)
-    spread_start(s.full_r, 1)
+    spread_start(s.full_r, 1, back)
+    for a, arr in enumerate((s.gx, s.gu)):
+        cols_drain(arr, a)
+    spread_drain(s.full_n, 0)
+    sum_drain(0)
     spread_column(s.full_r, 1)
     out_cross()
-    spread_across(s.full_r, 1)
-    spread_take(s.full_r, 1)
-    rows_of(s.full_r, r_rows)
+    for p in range(PARTS):
+        spread_across(s.full_r, 1, p)
+        spread_take(s.full_r, 1, p)
+        rows_of(s.full_r, r_rows, p)
+        if p < PARTS - 1:
+            at_cols = slice(p * part_width, (p + 1) * part_width)
+            for t in range(n_deep):
+                cols = pl.ds(t * deep, deep)
+                g = mm(r_rows[:, at_cols], s.dic_t[at_cols, cols])
+                s.g_sum[:, cols] = g + s.g_sum[:, cols] if p else g
     for t in range(n_deep):
         cols = pl.ds(t * deep, deep)
-        grad = mm_t(r_rows[...], s.dic[cols, :])
+        grad = mm(r_rows[:, last], s.dic_t[last, cols])
+        if PARTS > 1:
+            grad = grad + s.g_sum[:, cols]
         left[pl.ds(rows, rows), cols] = jnp.where(s.pre[:, cols] > 0.0, grad, 0.0).astype(BF16)
 
     out_final()
-    for a, arr in enumerate((s.gx, s.gu)):
-        cols_drain(arr, a)
-    for a, full in enumerate((s.full_n, s.full_r)):
-        spread_drain(full, a)
-    for a in range(2):
-        sum_drain(a)
+    spread_drain(s.full_r, 1)
+    sum_drain(1)
     out_drain()
 
 
@@ -519,6 +547,8 @@
         ebias=V((1, units), F32), dbias=V((width,), F32), gain=V((width,), F32),
         dic=V((units, width), BF16), gate=V((units, width), BF16),
         up=V((units, width), BF16), down=V((units, width), BF16),
+        dic_t=V((width, units), BF16), gate_t=V((width, units), BF16), up_t=V((width, units), BF16),
+        g_sum=V((rows, units), F32), u_sum=V((rows, units), F32),
         gx=V((n_dev, high, LANES), BF16), gu=V((n_dev, high, LANES), BF16),
         full_x=V((C, R, width), BF16), full_n=V((C, R, width), BF16), full_r=V((C, R, width), BF16),
         u_rows=V((rows, width), BF16), n_rows=V((rows, width), BF16),
@@ -533,7 +563,7 @@
         rbuf_out=V((Z, high, LANES), BF16), acc_out=V((high, LANES), F32),
         load_sem=D((9,)),
         col_ss=D((2,)), col_rs=D((2, L)), col_fs=D((2,)), col_fr=D((2,)),
-        ag_ss=D((2, 2)), ag_xs=D((2,)), ag_xr=D((2, Z + 1)), ag_rr=D((2, Z + 1)), ag_fs=D((2,)), ag_fr=D((2,)),
+        ag_ss=D((2, 2)), ag_xs=D((2,)), ag_xr=D((2, Z + 1, PARTS)), ag_rr=D((2, Z + 1, PARTS)), ag_fs=D((2,)), ag_fr=D((2, PARTS)),
         rs_cs=D((2,)), rs_cr=D((2,)), rs_ss=D((2,)), rs_rr=D((2, 2)), rs_xs=D((2,)), rs_xr=D((2, Z + 1)),
         out_cs=D((1,)), out_cr=D((1,)), out_xs=D((1,)), out_xr=D((Z,)), out_ss=D((1,)), out_rr=D((1,)),
     )
@@ -592,7 +622,7 @@
     rest = own_width - LANES
     if H != 2 or rows % (ROWS * H) or rows % PACK or width % LANES or units % LANES or units != units_mlp:
         return False
-    if rest <= 0 or rest >= LANES or LANES % rest or own_width * L * H != width:
+    if rest <= 0 or rest >= LANES or LANES % rest or own_width * L * H != width or width % (PARTS * LANES):
         return False
     return L == 8 and rows // ROWS // H == L + 1
 

time: 64.3 us -> 62.8 us (0.977)
  Pallas kernels: 63.5 us -> 62 us
    pallas_call x1, Pallas kernels: 60.4 us -> 58.9 us  [run_group(): pl.pallas_call(body, name='group_step', out_shape=(V((rows, own_width), B...]
where the time goes in v4:
time: 62.8 us; the launch traced here: 62.6 us
  Pallas kernels  62 us (99%)
  between operations  0.64 us (1%)
    pallas_call x1, Pallas kernels, run_group(): pl.pallas_call(body, name='group_step', out_shape=(V((rows, own_width), B...  58.9 us
    pallas_call x1, Pallas kernels, run_group(): pl.pallas_call(product, name='dictionary_product', out_shape=(jax.ShapeDt...  3.06 us

profile of v4, /device:TPU:0, one launch (start us, length us, event | category | flops | bytes accessed | tf_op | source)
XLA Modules:
  0.0 62.6 jit_solution(17940158418767859352)
XLA Ops:
  0.6 58.9 %group_step.1 = (bf16[144,144]{1,0:T(8,128)(2,1)S(1)}, bf16[288,512]{1,0:T(8,128)(2,1)S(1)}, bf16[288,2304]{1,0:T(8,128)(2,1)S(1)}) custom-call(s32[144,144]{1,0:T(8,128)} %refs_0_.1, s32[144,144]{1,0:T(8,128)} %refs_1_.1, bf16[512,2304]{1,0:T(8,128)(2,1)} %refs_2_.1, f32[1,512]{1,0:T(1,128)} %bitcast.1, f32[2304]{0:T(1024)} %refs_4_.1, f32[2304]{0:T(1024)} %refs_5_.1, ...), custom_call_target="tpu_custom_call" | custom-call | tf_op jit(solution)/shard_map/group_step/pallas_call | solution.py:577
  59.6 3.1 %dictionary_product.1 = (bf16[144,144]{1,0:T(8,128)(2,1)}, bf16[512,2304]{1,0:T(8,128)(2,1)}) custom-call(bf16[144,144]{1,0:T(8,128)(2,1)S(1)} %get-tuple-element.5.cols, bf16[288,512]{1,0:T(8,128)(2,1)S(1)} %get-tuple-element.6.left, bf16[288,2304]{1,0:T(8,128)(2,1)S(1)} %get-tuple-element.7.right), custom_call_target="tpu_custom_call" | custom-call | tf_op jit(solution)/shard_map/dictionary_product/pallas_call | solution.py:607

commit v5 on v4

--- a/solution.py
+++ b/solution.py
@@ -61,13 +61,24 @@
             def _():
                 body(1, L)
 
+    X = 2
+    Z = L // X
+    z, x = me // X, lax.rem(me, X)
+    across_me = z * X + 1 - x
+    near_z, same_z, flip_z = z + 1 - 2 * lax.rem(z, 2), z + 2 - 4 * (z // 2), 3 - z
+    peers = (near_z, same_z, flip_z)
+    far = (same_z, flip_z, near_z)
+
+    def col(zz):
+        return zz * X + x
+
+    def beside(zz):
+        return zz * X + 1 - x
+
     barrier = pltpu.get_barrier_semaphore()
-    for j in range(L):
-        for i in range(H):
-            if i or j:
-                pl.semaphore_signal(
-                    barrier, inc=1, device_id=at(lax.rem(me + j, L), lax.rem(h + i, H)), device_id_type=MESH
-                )
+    greeted = [(me, other), (across_me, h)] + [(col(zz), h) for zz in far]
+    for lat, hid in greeted:
+        pl.semaphore_signal(barrier, inc=1, device_id=at(lat, hid), device_id_type=MESH)
 
     loads = []
     for i, (src, dst) in enumerate((
@@ -90,20 +101,6 @@
                 part = pltpu.roll(part, (g % per) * rest, 1) if g % per else part
                 packed = part if packed is None else packed + part
             arr[mine, pl.ds(rows + b * PACK, PACK)] = packed.astype(BF16)
-
-    X = 2
-    Z = L // X
-    z, x = me // X, lax.rem(me, X)
-    across_me = z * X + 1 - x
-    near_z, same_z, flip_z = z + 1 - 2 * lax.rem(z, 2), z + 2 - 4 * (z // 2), 3 - z
-    peers = (near_z, same_z, flip_z)
-    far = (same_z, flip_z, near_z)
-
-    def col(zz):
-        return zz * X + x
-
-    def beside(zz):
-        return zz * X + 1 - x
 
     ext_z = ext(h) // X
     ext_here = lax.rem(ext(h), X) == x
@@ -394,7 +391,7 @@
 
     loads[0].wait()
     stage(s.codes_x, s.gx)
-    pl.semaphore_wait(barrier, n_dev - 1)
+    pl.semaphore_wait(barrier, len(greeted))
     cols_start(s.gx, 0)
     loads[1].wait()
     stage(s.codes_u, s.gu)

time: 62.8 us -> 61.2 us (0.975)
  Pallas kernels: 62 us -> 60.4 us
    pallas_call x1, Pallas kernels: 58.9 us -> 57.3 us  [run_group(): pl.pallas_call(body, name='group_step', out_shape=(V((rows, own_width), B...]
where the time goes in v5:
time: 61.2 us; the launch traced here: 61 us
  Pallas kernels  60.4 us (99%)
  between operations  0.64 us (1%)
    pallas_call x1, Pallas kernels, run_group(): pl.pallas_call(body, name='group_step', out_shape=(V((rows, own_width), B...  57.3 us
    pallas_call x1, Pallas kernels, run_group(): pl.pallas_call(product, name='dictionary_product', out_shape=(jax.ShapeDt...  3.06 us

profile of v5, /device:TPU:0, one launch (start us, length us, event | category | flops | bytes accessed | tf_op | source)
XLA Modules:
  0.0 61.0 jit_solution(18269486546371750864)
XLA Ops:
  0.6 57.3 %group_step.1 = (bf16[144,144]{1,0:T(8,128)(2,1)S(1)}, bf16[288,512]{1,0:T(8,128)(2,1)S(1)}, bf16[288,2304]{1,0:T(8,128)(2,1)S(1)}) custom-call(s32[144,144]{1,0:T(8,128)} %refs_0_.1, s32[144,144]{1,0:T(8,128)} %refs_1_.1, bf16[512,2304]{1,0:T(8,128)(2,1)} %refs_2_.1, f32[1,512]{1,0:T(1,128)} %bitcast.1, f32[2304]{0:T(1024)} %refs_4_.1, f32[2304]{0:T(1024)} %refs_5_.1, ...), custom_call_target="tpu_custom_call" | custom-call | tf_op jit(solution)/shard_map/group_step/pallas_call | solution.py:574
  58.0 3.1 %dictionary_product.1 = (bf16[144,144]{1,0:T(8,128)(2,1)}, bf16[512,2304]{1,0:T(8,128)(2,1)}) custom-call(bf16[144,144]{1,0:T(8,128)(2,1)S(1)} %get-tuple-element.5.cols, bf16[288,512]{1,0:T(8,128)(2,1)S(1)} %get-tuple-element.6.left, bf16[288,2304]{1,0:T(8,128)(2,1)S(1)} %get-tuple-element.7.right), custom_call_target="tpu_custom_call" | custom-call | tf_op jit(solution)/shard_map/dictionary_product/pallas_call | solution.py:604

commit v6 on v5

--- a/solution.py
+++ b/solution.py
@@ -206,6 +206,8 @@
                 piece = part(full, c, p)
                 for zz in far:
                     rcopy(piece, piece, s.ag_ss.at[a, slot], s.ag_rr.at[a, i, p], col(zz), h).start()
+                    if slot:
+                        rcopy(piece, piece, s.ag_ss.at[a, slot], s.ag_xr.at[a, i, p], beside(zz), h).start()
                 step_across(full, a, k, i, p)
                 hand_over(full, a, k, p)
 
@@ -224,7 +226,12 @@
         for p in range(PARTS):
             for zz in peers:
                 relay_column(full, a, col(zz), zz, p)
-            when_extra(ext_passes, lambda k, i: relay_column(full, a, k, i, p))
+
+            def passing(k, i):
+                wait_here(part(full, h * K + k, p), s.ag_rr.at[a, i, p])
+                hand_over(full, a, k, p)
+
+            when_extra(ext_passes, passing)
 
     def spread_across(full, a, p):
         relay_across(full, a, across_me, z, p)
@@ -245,8 +252,8 @@
             body(no)
 
     def spread_drain(full, a):
-        slots(lambda slot, k: wait_sent(full.at[pl.ds(0, Z - 1)], s.ag_ss.at[a, slot]))
-        either(ext_here, lambda n: wait_sent(full.at[pl.ds(0, n)], s.ag_xs.at[a]), Z, Z + 1)
+        slots(lambda slot, k: wait_sent(full.at[pl.ds(0, (slot + 1) * (Z - 1))], s.ag_ss.at[a, slot]))
+        either(ext_mine, lambda n: wait_sent(full.at[pl.ds(0, n)], s.ag_xs.at[a]), Z, Z + 1)
         wait_sent(full.at[pl.ds(0, K)], s.ag_fs.at[a])
 
     def rows_of(full, dst, p):
@@ -406,7 +413,6 @@
 
     def put_x(t, value):
         right[pl.ds(rows, rows), t * LANES : (t + 1) * LANES] = value.astype(BF16)
-        s.full_x[:, :, t * LANES : (t + 1) * LANES] = value.reshape(C, ROWS, LANES).astype(BF16)
 
     cols_rows(s.gx, put_x)
     loads[3].wait()
@@ -419,6 +425,7 @@
         sum_tile(0, t, mm(left[pl.ds(0, rows), :], s.dic[:, t * wide : (t + 1) * wide]))
     sum_start(0)
     sum_middle(0)
+    s.full_x[...] = x_rows[...].astype(F32).reshape(C, ROWS, width).astype(BF16)
     loads[7].wait()
     flip(s.gate, s.gate_t)
     loads[8].wait()
@@ -441,13 +448,13 @@
 
     spread_start(s.full_n, 0, norm)
     cols_across(s.gu, 1)
+    spread_column(s.full_n, 0)
     cols_take(s.gu, 1)
     cols_rows(s.gu, put_u)
     loads[6].wait()
     for t in range(n_deep):
         cols = pl.ds(t * deep, deep)
         s.hgrad[:, cols] = mm_t(s.u_rows[...], s.down[cols, :])
-    spread_column(s.full_n, 0)
     for p in range(PARTS):
         spread_across(s.full_n, 0, p)
         spread_take(s.full_n, 0, p)
@@ -589,7 +596,8 @@
     n_step = width // step
 
     def product(cols, left, right, block, grad, tiles, sem):
-        copies = []
+        copies = [pltpu.make_async_copy(cols, block, sem.at[n_step])]
+        copies[0].start()
         for t in range(n_step):
             at = slice(t * step, (t + 1) * step)
             tiles[t] = lax.dot_general(
@@ -597,7 +605,6 @@
             ).astype(BF16)
             copies.append(pltpu.make_async_copy(tiles.at[t], grad.at[:, at], sem.at[t]))
             copies[-1].start()
-        block[...] = cols[...]
         for cp in copies:
             cp.wait()
 
@@ -609,8 +616,8 @@
             jax.ShapeDtypeStruct((units, width), BF16),
         ),
         in_specs=[vm, vm, vm],
-        out_specs=(vm, pl.BlockSpec(memory_space=pl.ANY)),
-        scratch_shapes=[V((n_step, units, step), BF16), D((n_step,))],
+        out_specs=(pl.BlockSpec(memory_space=pl.ANY), pl.BlockSpec(memory_space=pl.ANY)),
+        scratch_shapes=[V((n_step, units, step), BF16), D((n_step + 1,))],
         compiler_params=pltpu.CompilerParams(vmem_limit_bytes=16 * 2**20),
     )(cols, left, right)
 

time: 61.2 us -> 60.1 us (0.982)
  Pallas kernels: 60.4 us -> 58.8 us
    pallas_call x1, Pallas kernels: 57.3 us -> 56.3 us  [run_group(): pl.pallas_call(body, name='group_step', out_shape=(V((rows, own_width), B...]
    pallas_call x1, Pallas kernels: 3.06 us -> 2.44 us  [run_group(): pl.pallas_call(product, name='dictionary_product', out_shape=(jax.ShapeDt...]
where the time goes in v6:
time: 60.1 us; the launch traced here: 59.4 us
  Pallas kernels  58.8 us (98%)
  between operations  0.64 us (1%)
    pallas_call x1, Pallas kernels, run_group(): pl.pallas_call(body, name='group_step', out_shape=(V((rows, own_width), B...  56.3 us
    pallas_call x1, Pallas kernels, run_group(): pl.pallas_call(product, name='dictionary_product', out_shape=(jax.ShapeDt...  2.44 us

profile of v6, /device:TPU:0, one launch (start us, length us, event | category | flops | bytes accessed | tf_op | source)
XLA Modules:
  0.0 59.4 jit_solution(3120710753937173677)
XLA Ops:
  0.6 56.3 %group_step.1 = (bf16[144,144]{1,0:T(8,128)(2,1)S(1)}, bf16[288,512]{1,0:T(8,128)(2,1)S(1)}, bf16[288,2304]{1,0:T(8,128)(2,1)S(1)}) custom-call(s32[144,144]{1,0:T(8,128)} %refs_0_.1, s32[144,144]{1,0:T(8,128)} %refs_1_.1, bf16[512,2304]{1,0:T(8,128)(2,1)} %refs_2_.1, f32[1,512]{1,0:T(1,128)} %bitcast.1, f32[2304]{0:T(1024)} %refs_4_.1, f32[2304]{0:T(1024)} %refs_5_.1, ...), custom_call_target="tpu_custom_call" | custom-call | tf_op jit(solution)/shard_map/group_step/pallas_call | solution.py:581
  57.0 2.4 %dictionary_product.1 = (bf16[144,144]{1,0:T(8,128)(2,1)}, bf16[512,2304]{1,0:T(8,128)(2,1)}) custom-call(bf16[144,144]{1,0:T(8,128)(2,1)S(1)} %get-tuple-element.5.cols, bf16[288,512]{1,0:T(8,128)(2,1)S(1)} %get-tuple-element.6.left, bf16[288,2304]{1,0:T(8,128)(2,1)S(1)} %get-tuple-element.7.right), custom_call_target="tpu_custom_call" | custom-call | tf_op jit(solution)/shard_map/dictionary_product/pallas_call | solution.py:611

commit v7 on v6

--- a/solution.py
+++ b/solution.py
@@ -388,7 +388,7 @@
     def mm(x, w):
         return lax.dot_general(x, w, (((1,), (0,)), ((), ())), preferred_element_type=F32)
 
-    deep = TILE if units % TILE == 0 else units
+    deep = units
     n_deep = units // deep
 
     def flip(src, dst):
@@ -512,6 +512,7 @@
     sum_drain(0)
     spread_column(s.full_r, 1)
     out_cross()
+    sum_drain(1)
     for p in range(PARTS):
         spread_across(s.full_r, 1, p)
         spread_take(s.full_r, 1, p)
@@ -531,7 +532,6 @@
 
     out_final()
     spread_drain(s.full_r, 1)
-    sum_drain(1)
     out_drain()
 
 

time: 60.1 us -> 59.9 us (level)
  no operation moved by 1% of the time
where the time goes in v7:
time: 59.9 us; the launch traced here: 59.3 us
  Pallas kernels  58.6 us (98%)
  between operations  0.64 us (1%)
    pallas_call x1, Pallas kernels, run_group(): pl.pallas_call(body, name='group_step', out_shape=(V((rows, own_width), B...  56.2 us
    pallas_call x1, Pallas kernels, run_group(): pl.pallas_call(product, name='dictionary_product', out_shape=(jax.ShapeDt...  2.44 us

profile of v7, /device:TPU:0, one launch (start us, length us, event | category | flops | bytes accessed | tf_op | source)
XLA Modules:
  0.0 59.3 jit_solution(8763840419409677401)
XLA Ops:
  0.6 56.2 %group_step.1 = (bf16[144,144]{1,0:T(8,128)(2,1)S(1)}, bf16[288,512]{1,0:T(8,128)(2,1)S(1)}, bf16[288,2304]{1,0:T(8,128)(2,1)S(1)}) custom-call(s32[144,144]{1,0:T(8,128)} %refs_0_.1, s32[144,144]{1,0:T(8,128)} %refs_1_.1, bf16[512,2304]{1,0:T(8,128)(2,1)} %refs_2_.1, f32[1,512]{1,0:T(1,128)} %bitcast.1, f32[2304]{0:T(1024)} %refs_4_.1, f32[2304]{0:T(1024)} %refs_5_.1, ...), custom_call_target="tpu_custom_call" | custom-call | tf_op jit(solution)/shard_map/group_step/pallas_call | solution.py:581
  56.8 2.4 %dictionary_product.1 = (bf16[144,144]{1,0:T(8,128)(2,1)}, bf16[512,2304]{1,0:T(8,128)(2,1)}) custom-call(bf16[144,144]{1,0:T(8,128)(2,1)S(1)} %get-tuple-element.5.cols, bf16[288,512]{1,0:T(8,128)(2,1)S(1)} %get-tuple-element.6.left, bf16[288,2304]{1,0:T(8,128)(2,1)S(1)} %get-tuple-element.7.right), custom_call_target="tpu_custom_call" | custom-call | tf_op jit(solution)/shard_map/dictionary_product/pallas_call | solution.py:611
